TPU v7x, 256 devices: a whole 4x4x8 slice. The times are simulated.
256 devices in a mesh: ep: 128 (over y, x, z), rep: 2 (over core).
Axes of the slice: x: 4, y: 4, z: 8, core: 2. Of those that a mesh axis runs over, the one named last changes fastest.
Arguments:
- dy: bfloat16 [4096, 2048], P('ep'), may hold values from -6 to 6
- probs: float32 [4096, 8], P('ep'), may hold values from 0.02 to 0.5
- expert_ids: int32 [4096, 8], P('ep'), may hold values from 0 to 127, as said below
- copy_choice: int32 [4096, 8], P('ep'), may hold values from 0 to 1, as said below
- saved_inputs: bfloat16 [128, 2, 128, 2, 2048], P('ep', 'rep'), may hold values from -24 to 24
- saved_gate: bfloat16 [128, 2, 128, 2, 768], P('ep', 'rep'), may hold values from -4 to 4
- saved_up: bfloat16 [128, 2, 128, 2, 768], P('ep', 'rep'), may hold values from -12 to 12
- down_weight: bfloat16 [128, 768, 2048], P('ep', None, 'rep'), may hold values from -4 to 4
- gate_weight: bfloat16 [128, 2048, 768], P('ep', 'rep'), may hold values from -4 to 4
- up_weight: bfloat16 [128, 2048, 768], P('ep', 'rep'), may hold values from -4 to 4
- new_owner: int32 [128], replicated, may hold values from 0 to 127, each once
Outputs:
- new_gate: bfloat16 [128, 2048, 768], P('ep', 'rep')
- new_up: bfloat16 [128, 2048, 768], P('ep', 'rep')
Inputs may be any that keep to these rules, and one draw needn't show every extreme that they name: `expert_ids`: each row names 8 different experts; the rows of one index of ep name each expert at most 2 * 2 times. `copy_choice`: of the pairs of the rows of one index of ep that name one expert, at most 2 take each copy; some take exactly 2 in every draw. `new_owner`: each expert has exactly one owner.
All inputs are finite; a program needn't handle non-finite values.
Results may differ from a plain program's by a relative error of at most 0.0056.
Values may be sent and summed in bfloat16 or wider, within the bound.
A program may use at most 64 MiB of HBM per device.

v0:
```python
import functools
import math

import jax
import jax.numpy as jnp
from jax import lax
from jax.experimental import pallas as pl
from jax.experimental.pallas import tpu as pltpu
from jax.sharding import PartitionSpec as P

MESH = pl.DeviceIdType.MESH
ITERS = 2

quintic_first = 3.4445
quintic_second = -4.775
quintic_third = 2.0315
step_scale = 2.0
epsilon = 1e-07

GRID = (4, 4, 8)


def shifted(me, k):
    ny, nx, nz = GRID
    y, x, z = me // (nx * nz), (me // nz) % nx, me % nz
    dy, dx, dz = k // (nx * nz), (k // nz) % nx, k % nz
    return (lax.rem(y + dy, ny) * nx + lax.rem(x + dx, nx)) * nz + lax.rem(z + dz, nz)


def greet(n, me):
    barrier = pltpu.get_barrier_semaphore()

    def say(k, carry):
        pl.semaphore_signal(barrier, inc=1, device_id={"ep": shifted(me, k)}, device_id_type=MESH)
        return carry

    lax.fori_loop(1, n, say, 0)
    pl.semaphore_wait(barrier, n - 1)


def from_partner(block):
    return lax.ppermute(block, "rep", [(0, 1), (1, 0)])


def dot(a, b, dims):
    return lax.dot_general(a, b, (dims, ((), ())), preferred_element_type=jnp.float32)


def exchange_kernel(n, x_ref, o_ref, send, recv, local):
    me = lax.axis_index("ep")
    greet(n, me)
    own = pltpu.make_async_copy(x_ref.at[me], o_ref.at[me], local)
    own.start()

    def go(k, carry):
        to = shifted(me, k)
        pltpu.make_async_remote_copy(
            src_ref=x_ref.at[to], dst_ref=o_ref.at[me], send_sem=send, recv_sem=recv,
            device_id={"ep": to}, device_id_type=MESH,
        ).start()
        return carry

    lax.fori_loop(1, n, go, 0)
    own.wait()
    rest = pl.ds(0, n - 1)
    everything = pltpu.make_async_remote_copy(
        src_ref=x_ref.at[rest], dst_ref=o_ref.at[rest], send_sem=send, recv_sem=recv,
        device_id={"ep": shifted(me, 1)}, device_id_type=MESH,
    )
    everything.wait_send()
    everything.wait_recv()


def exchange(x):
    n = x.shape[0]
    return pl.pallas_call(
        functools.partial(exchange_kernel, n),
        out_shape=jax.ShapeDtypeStruct(x.shape, x.dtype),
        in_specs=[pl.BlockSpec(memory_space=pl.ANY)],
        out_specs=pl.BlockSpec(memory_space=pl.ANY),
        scratch_shapes=[pltpu.SemaphoreType.DMA] * 3,
        compiler_params=pltpu.CompilerParams(collective_id=1, has_side_effects=True),
        name="exchange",
    )(x)


def orthogonal_factor(kernel_matrix, rows):
    high = kernel_matrix.astype(jnp.bfloat16)
    low = (kernel_matrix - high.astype(jnp.float32)).astype(jnp.bfloat16)
    product = dot(high, rows, ((1,), (0,))) + dot(low, rows, ((1,), (0,)))
    total = jnp.sqrt(jnp.maximum(jnp.sum(rows.astype(jnp.float32) * product), 0.0))
    scale = 1.0 / (total + epsilon)
    product = product * (scale * scale)
    for repeat in range(ITERS):
        if repeat:
            product = dot(high, rows, ((1,), (0,))) + dot(low, rows, ((1,), (0,)))
        gram = dot(rows, product.astype(jnp.bfloat16), ((0,), (0,)))
        half = gram.astype(jnp.bfloat16)
        square = dot(half, half, ((1,), (0,)))
        poly = (quintic_second * gram + quintic_third * square).astype(jnp.bfloat16)
        mixed = quintic_first * rows.astype(jnp.float32) + dot(rows, poly, ((1,), (0,)))
        if not repeat:
            mixed = mixed * scale
        rows = mixed.astype(jnp.bfloat16)
    return rows


def move_kernel(
    n, factor, inverse, k_ref, r_ref, x_ref, gate_ref, up_ref, own_out, other_out,
    weights, factors, made0, made1, held0, held1, ready0, ready1, load, send, recv, local, swap,
):
    me = lax.axis_index("ep")
    core = lax.axis_index("rep")
    outs, made, held, ready = (own_out, other_out), (made0, made1), (held0, held1), (ready0, ready1)
    ny = GRID[0]
    group = n // ny
    piece = weights.shape[1] // n
    block = group * piece
    rest = pl.ds(0, n - 1)
    partner = {"rep": 1 - core}

    barrier = pltpu.get_barrier_semaphore()

    def say(k, carry):
        pl.semaphore_signal(barrier, inc=1, device_id={"ep": shifted(me, k)}, device_id_type=MESH)
        return carry

    lax.fori_loop(1, n, say, 0)
    pl.semaphore_signal(barrier, inc=1, device_id=partner, device_id_type=MESH)

    for c, refs in enumerate(((gate_ref, up_ref), (up_ref, gate_ref))):
        @pl.when(core == c)
        def _(refs=refs):
            for q in range(2):
                pltpu.make_async_copy(refs[q], weights.at[q], load.at[q]).start()

    factors[0] = orthogonal_factor(k_ref[...], r_ref[...])
    pl.semaphore_wait(barrier, n)
    trade = pltpu.make_async_remote_copy(
        src_ref=factors.at[0], dst_ref=factors.at[1], send_sem=swap.at[0], recv_sem=swap.at[1],
        device_id=partner, device_id_type=MESH,
    )
    trade.start()

    for q in range(2):
        pltpu.make_async_copy(gate_ref, weights.at[q], load.at[q]).wait()
        if q:
            trade.wait_recv()

        def spread(k, carry, q=q):
            to = shifted(me, k)
            pltpu.make_async_remote_copy(
                src_ref=made[q].at[to], dst_ref=held[q].at[me], send_sem=send.at[q], recv_sem=recv.at[q],
                device_id={"ep": to}, device_id_type=MESH,
            ).start()
            return carry

        def produce(dy, carry, q=q):
            y = lax.rem(me // group + dy, ny)
            rows = pl.ds(pl.multiple_of(y * block, block), block)
            ortho = dot(x_ref[:, rows], factors[q], ((0,), (0,)))
            fresh = (weights[q, rows, :].astype(jnp.float32) - factor * ortho).astype(jnp.bfloat16)
            made[q][pl.ds(y * group, group)] = fresh.reshape(group, piece, fresh.shape[1])
            lax.fori_loop(jnp.where(dy == 0, 1, dy * group), (dy + 1) * group, spread, 0)
            return carry

        lax.fori_loop(0, ny, produce, 0)
        pltpu.make_async_copy(made[q].at[me], held[q].at[me], local.at[q]).start()

    for q in range(2):
        pltpu.make_async_copy(made[q].at[me], held[q].at[me], local.at[q]).wait()
        pltpu.make_async_remote_copy(
            src_ref=made[q].at[rest], dst_ref=held[q].at[rest], send_sem=send.at[q], recv_sem=recv.at[q],
            device_id={"ep": shifted(me, 1)}, device_id_type=MESH,
        ).wait_recv()

        def collect(k, carry, q=q):
            to = shifted(me, k)
            ready[q][k] = held[q][inverse[to]]
            pltpu.make_async_remote_copy(
                src_ref=ready[q].at[k], dst_ref=outs[q].at[me], send_sem=send.at[2 + q], recv_sem=recv.at[2 + q],
                device_id={"ep": to}, device_id_type=MESH,
            ).start()
            return carry

        lax.fori_loop(1, n, collect, 0)
        ready[q][0] = held[q][inverse[me]]
        pltpu.make_async_copy(ready[q].at[0], outs[q].at[me], local.at[2 + q]).start()

    trade.wait_send()
    for q in range(2):
        pltpu.make_async_copy(ready[q].at[0], outs[q].at[me], local.at[2 + q]).wait()
        pltpu.make_async_remote_copy(
            src_ref=made[q].at[rest], dst_ref=held[q].at[rest], send_sem=send.at[q], recv_sem=recv.at[q],
            device_id={"ep": shifted(me, 1)}, device_id_type=MESH,
        ).wait_send()
        last = pltpu.make_async_remote_copy(
            src_ref=ready[q].at[rest], dst_ref=outs[q].at[rest], send_sem=send.at[2 + q], recv_sem=recv.at[2 + q],
            device_id={"ep": shifted(me, 1)}, device_id_type=MESH,
        )
        last.wait_send()
        last.wait_recv()


def move(n, factor, inverse, kernel_matrix, rows, columns, gate, up):
    half, inner = gate.shape
    pieces = (n, half // n, inner)
    shape = jax.ShapeDtypeStruct(pieces, gate.dtype)
    everywhere, vmem = pl.BlockSpec(memory_space=pl.ANY), pl.BlockSpec(memory_space=pltpu.VMEM)
    return pl.pallas_call(
        functools.partial(move_kernel, n, factor),
        out_shape=(shape, shape),
        in_specs=[pl.BlockSpec(memory_space=pltpu.SMEM), vmem, vmem, vmem, everywhere, everywhere],
        out_specs=(everywhere, everywhere),
        scratch_shapes=[
            pltpu.VMEM((2, half, inner), gate.dtype),
            pltpu.VMEM((2,) + rows.shape, rows.dtype),
        ]
        + [pltpu.VMEM(pieces, gate.dtype)] * 6
        + [
            pltpu.SemaphoreType.DMA((2,)),
            pltpu.SemaphoreType.DMA((4,)),
            pltpu.SemaphoreType.DMA((4,)),
            pltpu.SemaphoreType.DMA((4,)),
            pltpu.SemaphoreType.DMA((2,)),
        ],
        compiler_params=pltpu.CompilerParams(
            collective_id=2, has_side_effects=True, vmem_limit_bytes=48 * 2**20
        ),
        name="move",
    )(inverse, kernel_matrix, rows, columns, gate, up)


def shards(
    dy,
    probs,
    expert_ids,
    copy_choice,
    saved_inputs,
    saved_gate,
    saved_up,
    down_weight,
    gate_weight,
    up_weight,
    new_owner,
):
    copy_index = lax.axis_index("rep")
    experts = lax.axis_size("ep")
    capacity = saved_inputs.shape[3]
    tokens, width = dy.shape
    inner = saved_gate.shape[4]
    half = width // 2
    first = copy_index == 0

    expert = jnp.arange(experts, dtype=jnp.int32)
    hits = (expert_ids[:, :, None] == expert) & (copy_choice == copy_index)[:, :, None]
    chosen = jnp.any(hits, axis=1)
    weight = jnp.sum(jnp.where(hits, probs[:, :, None], 0.0), axis=1)
    before = jnp.tril(jnp.ones((tokens, tokens), jnp.bfloat16), -1)
    position = jnp.dot(before, chosen.astype(jnp.bfloat16), preferred_element_type=jnp.float32)
    slot = jnp.arange(capacity, dtype=jnp.float32)
    select = chosen[:, :, None] & (position[:, :, None] == slot)
    scale = jnp.sum(jnp.where(select, weight[:, :, None], 0.0), axis=0)
    rows = lax.dot_general(
        select.astype(jnp.bfloat16), dy, (((0,), (0,)), ((), ())), preferred_element_type=jnp.float32
    )
    outgoing = (scale[:, :, None] * rows).astype(jnp.bfloat16)
    routed = exchange(outgoing).reshape(experts * capacity, width)

    def ordered(own, other, axis):
        return jnp.where(first, jnp.concatenate([own, other], axis), jnp.concatenate([other, own], axis))

    down = down_weight[0]
    hidden_grad = dot(routed, ordered(down, from_partner(down), 1), ((1,), (1,))) / math.sqrt(inner)
    gate_value = saved_gate.reshape(-1, inner).astype(jnp.float32)
    up_value = saved_up.reshape(-1, inner).astype(jnp.float32)
    sigmoid = jax.nn.sigmoid(gate_value)
    gate_rows = (hidden_grad * up_value * sigmoid * (1.0 + gate_value * (1.0 - sigmoid))).astype(jnp.bfloat16)
    up_rows = (hidden_grad * gate_value * sigmoid).astype(jnp.bfloat16)
    own_rows = jnp.where(first, gate_rows, up_rows)
    other_rows = from_partner(jnp.where(first, up_rows, gate_rows))
    factor_rows = ordered(own_rows, other_rows, 0)

    inputs = saved_inputs.reshape(-1, width)
    all_inputs = ordered(inputs, from_partner(inputs), 0)
    kernel_matrix = dot(all_inputs, all_inputs, ((1,), (1,)))
    columns = jnp.where(first, all_inputs[:, :half], all_inputs[:, half:])
    inverse = jnp.sum(
        jnp.where(new_owner[:, None] == expert[None, :], expert[:, None], 0), axis=0, dtype=jnp.int32
    )
    own, other = move(
        experts, step_scale * math.sqrt(width), inverse, kernel_matrix, factor_rows, columns, gate_weight[0], up_weight[0]
    )
    new_gate, new_up = jnp.where(first, own, other), jnp.where(first, other, own)
    return new_gate.reshape(1, half, inner), new_up.reshape(1, half, inner)


def solution(mesh):
    in_specs = (
        P("ep", None),
        P("ep", None),
        P("ep", None),
        P("ep", None),
        P("ep", "rep", None, None, None),
        P("ep", "rep", None, None, None),
        P("ep", "rep", None, None, None),
        P("ep", None, "rep"),
        P("ep", "rep", None),
        P("ep", "rep", None),
        P(),
    )
    out_specs = (P("ep", "rep", None), P("ep", "rep", None))
    return jax.shard_map(shards, mesh=mesh, in_specs=in_specs, out_specs=out_specs, check_vma=False)
```

profile of v0, /device:TPU:1, one launch (start us, length us, event | category | flops | bytes accessed | tf_op | source)
XLA Modules:
  0.0 218.4 jit_solution(12526475933095005275)
XLA Ops:
  0.7 3.3 %collective-permute-start.1 = (bf16[768,1024]{1,0:T(8,128)(2,1)}, bf16[768,1024]{1,0:T(8,128)(2,1)}, u32[]{:S(2)}, u32[]{:S(2)}) collective-permute-start(bf16[768,1024]{1,0:T(8,128)(2,1)} %bitcast.16), channel_id=1, source_target_pairs={{0,1},{1,0},{2,3},{3,2},{4,5},{5,4},{6,7},{7,6},{8,9},{9,8},{10,11... | collective-permute-start | bytes 4718600 | tf_op jit(solution)/shard_map/ppermute | solution.py:42
  4.0 1.5 reshape.30
  5.4 0.1 collective-permute-start
  5.8 0.2 fusion.10
  6.0 0.2 select_reduce_fusion
  6.2 0.2 fusion.16
  6.4 0.5 convolution_multiply_fusion
  6.9 2.0 copy.32.x_ref
  8.9 37.8 %exchange.1 = bf16[128,2,2048]{2,1,0:T(2,128)(2,1)} custom-call(bf16[128,2,2048]{2,1,0:T(2,128)(2,1)} %copy.32.x_ref), custom_call_target="tpu_custom_call" | custom-call | tf_op jit(solution)/shard_map/exchange/pallas_call | solution.py:76
  46.7 1.5 reshape.31
  48.2 2.0 reshape.34
  50.2 2.0 reshape.35
  52.2 0.1 select_reduce_fusion.1.inverse
  52.3 1.0 maximum_select_fusion.2
  53.3 0.1 slice_select_fusion.x_ref
  53.4 1.0 copy-done.1
  54.4 0.2 copy-done.2
  54.6 0.5 copy-done.6
  55.1 3.4 %broadcast_select_fusion.1 = (bf16[256,768]{1,0:T(8,128)(2,1)S(1)}, bf16[256,768]{1,0:T(8,128)(2,1)S(1)}, bf16[256,768]{1,0:T(8,128)(2,1)S(1)}) fusion(pred[]{:T(512)S(6)} %eq.48, f32[256,768]{1,0:T(8,128)S(1)} %copy-done.2, f32[256,768]{1,0:T(8,128)S(1)} %copy-done.1, bf16[256,2048]{1,0:T(8,128)(2,1)S(1)} %reshape.31, ...), kind=kOutput, calls=%fused_computation.20 | convolution fusion | flops 822411264 | bytes 6946817 | tf_op jit(solution)/shard_map/dot_general | solution.py:46
  58.6 2.1 collective-permute-start.2
  60.6 1.3 fusion.24.k_ref
  62.0 0.3 maximum_select_fusion.5.r_ref
  62.3 154.3 %move.1 = (bf16[128,8,768]{2,1,0:T(8,128)(2,1)S(1)}, bf16[128,8,768]{2,1,0:T(8,128)(2,1)S(1)}) custom-call(s32[128]{0:T(128)S(1)} %select_reduce_fusion.1.inverse, f32[512,512]{1,0:T(8,128)S(1)} %fusion.24.k_ref, bf16[512,768]{1,0:T(8,128)(2,1)S(1)} %maximum_select_fusion.5.r_ref, bf16[512,1024]{1,0:T(8,128)(2,1)S(1)} %slice_select_fusion.x_ref, ...), custom_call_target="tpu_custom_call" | custom-call | tf_op jit(solution)/shard_map/move/pallas_call | solution.py:210
  216.6 1.9 select_bitcast_fusion
  (23 shorter events, 0.4 us)
Async XLA Ops:
  0.6 5.8 %copy-start = (bf16[32,2048]{1,0:T(8,128)(2,1)S(1)}, bf16[32,2048]{1,0:T(8,128)(2,1)}, u32[]{:S(2)}) copy-start(bf16[32,2048]{1,0:T(8,128)(2,1)} %param.11) | copy-start | bytes 393220
  0.6 4.9 %copy-start.5 = (s32[32,8]{0,1:T(8,128)S(1)}, s32[32,8]{0,1:T(8,128)}, u32[]{:S(2)}) copy-start(s32[32,8]{0,1:T(8,128)} %param.14) | copy-start | bytes 3076
  0.7 5.0 %copy-start.3 = (s32[32,8]{0,1:T(8,128)S(1)}, s32[32,8]{0,1:T(8,128)}, u32[]{:S(2)}) copy-start(s32[32,8]{0,1:T(8,128)} %param.13) | copy-start | bytes 3076
  0.7 5.1 %copy-start.4 = (f32[32,8]{0,1:T(8,128)S(1)}, f32[32,8]{0,1:T(8,128)}, u32[]{:S(2)}) copy-start(f32[32,8]{0,1:T(8,128)} %param.12) | copy-start | bytes 3076
  0.7 52.7 %collective-permute-start.1 = (bf16[768,1024]{1,0:T(8,128)(2,1)}, bf16[768,1024]{1,0:T(8,128)(2,1)}, u32[]{:S(2)}, u32[]{:S(2)}) collective-permute-start(bf16[768,1024]{1,0:T(8,128)(2,1)} %bitcast.16), channel_id=1, source_target_pairs={{0,1},{1,0},{2,3},{3,2},{4,5},{5,4},{6,7},{7,6},{8,9},{9,8},{10,11... | collective-permute-start | bytes 4718600 | tf_op jit(solution)/shard_map/ppermute | solution.py:42
  5.4 46.8 %collective-permute-start = (bf16[256,2048]{1,0:T(8,128)(2,1)S(1)}, bf16[256,2048]{1,0:T(8,128)(2,1)S(1)}, u32[]{:S(2)}, u32[]{:S(2)}) collective-permute-start(bf16[256,2048]{1,0:T(8,128)(2,1)S(1)} %reshape.30), channel_id=1, source_target_pairs={{0,1},{1,0},{2,3},{3,2},{4,5},{5,4},{6,7},{7,6},{8,9},{9,8},{10,11... | collective-permute-start | bytes 3145736 | tf_op jit(solution)/shard_map/ppermute | solution.py:42
  46.7 5.5 %copy-start.7 = (s32[128]{0:T(128)S(1)}, s32[128]{0:T(128)}, u32[]{:S(2)}) copy-start(s32[128]{0:T(128)} %param.21) | copy-start | bytes 1540
  53.2 1.1 copy-start.1
  53.3 1.4 copy-start.2
  53.3 1.9 copy-start.6
  58.6 3.4 %collective-permute-start.2 = (bf16[256,768]{1,0:T(8,128)(2,1)S(1)}, bf16[256,768]{1,0:T(8,128)(2,1)S(1)}, u32[]{:S(2)}, u32[]{:S(2)}) collective-permute-start(bf16[256,768]{1,0:T(8,128)(2,1)S(1)} %broadcast_select_fusion), channel_id=1, source_target_pairs={{0,1},{1,0},{2,3},{3,2},{4,5},{5,4},{6,7},{7,6},{8,9},{9,8},{10,11... | collective-permute-start | bytes 1179656 | tf_op jit(solution)/shard_map/ppermute | solution.py:42
where the time goes:
time: 219 us; the launch traced here: 218 us
  Pallas kernels  192 us (88%)
  local copies, waits for them, and re-layouts  11 us (5%)
  starting transfers between devices  5.47 us (2%)
  matrix products  5.3 us (2%)
  other arithmetic  3.77 us (2%)
    pallas_call x1, Pallas kernels, move(): pl.pallas_call(functools.partial(move_kernel, n, factor), out_shape=(shap...  154 us
    pallas_call x1, Pallas kernels, exchange(): pl.pallas_call(functools.partial(exchange_kernel, n), out_shape=jax.Shape...  37.8 us
    ppermute x3, starting transfers between devices, from_partner(): return lax.ppermute(block, 'rep', [(0, 1), (1, 0)])  5.47 us
    dot_general x2, matrix products, dot(): lax.dot_general(a, b, (dims, ((), ())), preferred_element_type=jnp.float32)  4.63 us
  transfers between devices with their start and end apart: 3, of which 1 were waited for; matrix products, arithmetic and copies ran while one was open for 6% of the time, Pallas kernels for 17%

commit v1 on v0

--- a/solution.py
+++ b/solution.py
@@ -27,61 +27,245 @@
     return (lax.rem(y + dy, ny) * nx + lax.rem(x + dx, nx)) * nz + lax.rem(z + dz, nz)
 
 
-def greet(n, me):
-    barrier = pltpu.get_barrier_semaphore()
-
-    def say(k, carry):
-        pl.semaphore_signal(barrier, inc=1, device_id={"ep": shifted(me, k)}, device_id_type=MESH)
-        return carry
-
-    lax.fori_loop(1, n, say, 0)
-    pl.semaphore_wait(barrier, n - 1)
-
-
-def from_partner(block):
-    return lax.ppermute(block, "rep", [(0, 1), (1, 0)])
-
-
 def dot(a, b, dims):
     return lax.dot_general(a, b, (dims, ((), ())), preferred_element_type=jnp.float32)
 
 
-def exchange_kernel(n, x_ref, o_ref, send, recv, local):
+CHUNKS = 2
+
+
+def shift_of(size):
+    assert size & (size - 1) == 0
+    return size.bit_length() - 1
+
+
+def selection(key_columns, plane, top, sources, tokens, spots, capacity):
+    count = sources * tokens
+    lanes = 2 * spots * sources * capacity
+    lane = lax.broadcasted_iota(jnp.int32, (1, lanes), 1)
+    slot = lane & (capacity - 1)
+    source = (lane >> shift_of(capacity)) & (sources - 1)
+    spot = (lane >> shift_of(capacity * sources)) & (spots - 1)
+    copy = lane >> shift_of(capacity * sources * spots)
+    wanted = (((spot * sources + plane) * 2) + copy).astype(jnp.float32)
+    here = (lax.broadcasted_iota(jnp.int32, (count, 1), 0) >> shift_of(tokens)) == source
+    taken = jnp.zeros((count, lanes), jnp.float32)
+    weight = jnp.zeros((count, lanes), jnp.float32)
+    for k in range(top):
+        hit = (key_columns[:, k : k + 1] == wanted) & here
+        taken = jnp.where(hit, 1.0, taken)
+        weight = jnp.where(hit, key_columns[:, top + k : top + k + 1], weight)
+    row = lax.broadcasted_iota(jnp.int32, (count, count), 0)
+    column = lax.broadcasted_iota(jnp.int32, (count, count), 1)
+    before = jnp.where(row > column, 1.0, 0.0).astype(jnp.bfloat16)
+    position = dot(before, taken.astype(jnp.bfloat16), ((1,), (0,)))
+    mine = (taken > 0.5) & (position == slot.astype(jnp.float32))
+    ones = jnp.ones((count, 128), jnp.bfloat16)
+    left = jnp.where(mine, weight, 0.0)
+    scale = None
+    for _ in range(3):
+        part = left.astype(jnp.bfloat16)
+        left = left - part.astype(jnp.float32)
+        term = dot(part, ones, ((0,), (0,)))
+        scale = term if scale is None else scale + term
+    return jnp.where(mine, 1.0, 0.0).astype(jnp.bfloat16), scale
+
+
+def remote(src, dst, send, recv, to):
+    return pltpu.make_async_remote_copy(
+        src_ref=src, dst_ref=dst, send_sem=send, recv_sem=recv, device_id=to, device_id_type=MESH
+    )
+
+
+def route_kernel(
+    top, meta_ref, dy_ref, x_ref, g_ref, u_ref, down_ref, k_out, r_out, x_out,
+    line, keys, sent, routed, inputs, down, rows, other,
+    line_send, line_recv, keys_sem, plane_send, plane_recv, near_send, near_recv, pair_send, pair_recv,
+    own_sem, piece_sem,
+):
     me = lax.axis_index("ep")
-    greet(n, me)
-    own = pltpu.make_async_copy(x_ref.at[me], o_ref.at[me], local)
-    own.start()
-
-    def go(k, carry):
-        to = shifted(me, k)
-        pltpu.make_async_remote_copy(
-            src_ref=x_ref.at[to], dst_ref=o_ref.at[me], send_sem=send, recv_sem=recv,
-            device_id={"ep": to}, device_id_type=MESH,
+    core = lax.axis_index("rep")
+    nz = GRID[2]
+    spots = GRID[0] * GRID[1]
+    z, spot = me % nz, me // nz
+    tokens, width = line.shape[2], line.shape[3]
+    capacity = sent.shape[3] // nz
+    half = CHUNKS * width
+    partner = {"rep": 1 - core}
+
+    def above(k):
+        return {"ep": shifted(me, k)}
+
+    barrier = pltpu.get_barrier_semaphore()
+
+    def greet_line(k, carry):
+        pl.semaphore_signal(barrier, inc=1, device_id=above(k), device_id_type=MESH)
+        return carry
+
+    def greet_plane(k, carry):
+        for c in range(2):
+            pl.semaphore_signal(
+                barrier, inc=1, device_id={"ep": shifted(me, k * nz), "rep": c}, device_id_type=MESH
+            )
+        return carry
+
+    lax.fori_loop(1, nz, greet_line, 0)
+    lax.fori_loop(1, spots, greet_plane, 0)
+    pl.semaphore_signal(barrier, inc=1, device_id=partner, device_id_type=MESH)
+
+    def columns(chunk):
+        return pl.ds(pl.multiple_of(core * half + chunk * width, width), width)
+
+    own = [pltpu.make_async_copy(dy_ref.at[:, columns(h)], line.at[h, z], own_sem.at[h]) for h in range(CHUNKS)]
+    own.append(pltpu.make_async_copy(meta_ref, keys.at[z], own_sem.at[CHUNKS]))
+    own.append(pltpu.make_async_copy(x_ref, inputs.at[core], own_sem.at[CHUNKS + 1]))
+    own.append(pltpu.make_async_copy(down_ref, down.at[core], own_sem.at[CHUNKS + 2]))
+    for copy in own:
+        copy.start()
+    pl.semaphore_wait(barrier, nz + 2 * (spots - 1))
+
+    def send_keys(k, carry):
+        remote(meta_ref, keys.at[z], keys_sem.at[0], keys_sem.at[1], above(k)).start()
+        return carry
+
+    lax.fori_loop(1, nz, send_keys, 0)
+    for h in range(CHUNKS):
+
+        def send_line(k, carry, h=h):
+            remote(dy_ref.at[:, columns(h)], line.at[h, z], line_send.at[h], line_recv.at[h], above(k)).start()
+            return carry
+
+        lax.fori_loop(1, nz, send_line, 0)
+    swaps = [
+        remote(x_ref, inputs.at[core], pair_send.at[0], pair_recv.at[0], partner),
+        remote(down_ref, down.at[core], pair_send.at[1], pair_recv.at[1], partner),
+    ]
+    for swap in swaps:
+        swap.start()
+
+    others = pl.ds(0, nz - 1)
+    all_keys = remote(keys.at[others], keys.at[others], keys_sem.at[0], keys_sem.at[1], above(1))
+    all_keys.wait_recv()
+    own[CHUNKS].wait()
+    choose, scale = selection(
+        keys[...].reshape(nz * tokens, keys.shape[2]), z, top, nz, tokens, spots, capacity
+    )
+    scale = jnp.concatenate([scale] * (width // scale.shape[1]), axis=1)
+    for h in range(CHUNKS):
+        own[h].wait()
+        remote(line.at[h, others], line.at[h, others], line_send.at[h], line_recv.at[h], above(1)).wait_recv()
+        picked = dot(choose, line[h].reshape(nz * tokens, width), ((0,), (0,)))
+        sent[h] = (picked * scale).astype(jnp.bfloat16).reshape(sent.shape[1:])
+
+        def send_plane(k, carry, h=h):
+            to = shifted(me, k * nz)
+            for c in range(2):
+                remote(
+                    sent.at[h, c, to // nz], routed.at[spot, :, columns(h)],
+                    plane_send.at[h], plane_recv.at[h], {"ep": to, "rep": c},
+                ).start()
+            return carry
+
+        lax.fori_loop(1, spots, send_plane, 0)
+        remote(
+            sent.at[h, 1 - core, spot], routed.at[spot, :, columns(h)], near_send.at[h], near_recv.at[h], partner
         ).start()
-        return carry
-
-    lax.fori_loop(1, n, go, 0)
-    own.wait()
-    rest = pl.ds(0, n - 1)
-    everything = pltpu.make_async_remote_copy(
-        src_ref=x_ref.at[rest], dst_ref=o_ref.at[rest], send_sem=send, recv_sem=recv,
-        device_id={"ep": shifted(me, 1)}, device_id_type=MESH,
-    )
-    everything.wait_send()
-    everything.wait_recv()
-
-
-def exchange(x):
-    n = x.shape[0]
+        pltpu.make_async_copy(
+            sent.at[h, core, spot], routed.at[spot, :, columns(h)], piece_sem.at[h]
+        ).start()
+
+    own[CHUNKS + 1].wait()
+    swaps[0].wait_recv()
+    copies, pairs, features = inputs.shape
+    everything = inputs[...].reshape(copies * pairs, features)
+    k_out[...] = dot(everything, everything, ((1,), (1,)))
+    for c in range(2):
+        x_out[c] = inputs[c, :, pl.ds(pl.multiple_of(core * half, half), half)]
+    gate_value = g_ref[...].astype(jnp.float32).reshape(pairs, g_ref.shape[-1])
+    up_value = u_ref[...].astype(jnp.float32).reshape(pairs, u_ref.shape[-1])
+    own[CHUNKS + 2].wait()
+    swaps[1].wait_recv()
+    near = pl.ds(0, spots - 1)
+    for h in range(CHUNKS):
+        pltpu.make_async_copy(sent.at[h, core, spot], routed.at[spot, :, columns(h)], piece_sem.at[h]).wait()
+        remote(
+            sent.at[h, 1 - core, spot], routed.at[spot, :, columns(h)], near_send.at[h], near_recv.at[h], partner
+        ).wait_recv()
+        both = routed.at[near, :, pl.ds(h * 2 * width, 2 * width)]
+        remote(both, both, plane_send.at[h], plane_recv.at[h], partner).wait_recv()
+
+    arrived = routed[...].reshape(pairs, features)
+    hidden = dot(arrived[:, :half], down[0], ((1,), (1,))) + dot(arrived[:, half:], down[1], ((1,), (1,)))
+    hidden = hidden / math.sqrt(hidden.shape[1])
+    sigmoid = jax.nn.sigmoid(gate_value)
+    gate_rows = hidden * up_value * sigmoid * (1.0 + gate_value * (1.0 - sigmoid))
+    up_rows = hidden * gate_value * sigmoid
+    first = core == 0
+    rows[core] = jnp.where(first, gate_rows, up_rows).astype(jnp.bfloat16)
+    other[...] = jnp.where(first, up_rows, gate_rows).astype(jnp.bfloat16)
+    last = remote(other, rows.at[core], pair_send.at[2], pair_recv.at[2], partner)
+    last.start()
+
+    all_keys.wait_send()
+    for swap in swaps:
+        swap.wait_send()
+    for h in range(CHUNKS):
+        remote(line.at[h, others], line.at[h, others], line_send.at[h], line_recv.at[h], above(1)).wait_send()
+        remote(
+            sent.at[h, 1 - core, spot], routed.at[spot, :, columns(h)], near_send.at[h], near_recv.at[h], partner
+        ).wait_send()
+        both = sent.at[h, :, near]
+        remote(both, both, plane_send.at[h], plane_recv.at[h], partner).wait_send()
+    last.wait_send()
+    last.wait_recv()
+    r_out[...] = rows[...]
+
+
+def route(meta, dy, inputs, gate, up, down, top):
+    pairs, features = inputs.shape
+    inner, half = down.shape
+    tokens = dy.shape[0]
+    nz, spots = GRID[2], GRID[0] * GRID[1]
+    slots = pairs // spots
+    width = half // CHUNKS
+    everywhere, vmem = pl.BlockSpec(memory_space=pl.ANY), pl.BlockSpec(memory_space=pltpu.VMEM)
+    bf16 = jnp.bfloat16
+    semaphores = pltpu.SemaphoreType.DMA
     return pl.pallas_call(
-        functools.partial(exchange_kernel, n),
-        out_shape=jax.ShapeDtypeStruct(x.shape, x.dtype),
-        in_specs=[pl.BlockSpec(memory_space=pl.ANY)],
-        out_specs=pl.BlockSpec(memory_space=pl.ANY),
-        scratch_shapes=[pltpu.SemaphoreType.DMA] * 3,
-        compiler_params=pltpu.CompilerParams(collective_id=1, has_side_effects=True),
-        name="exchange",
-    )(x)
+        functools.partial(route_kernel, top),
+        out_shape=(
+            jax.ShapeDtypeStruct((2 * pairs, 2 * pairs), jnp.float32),
+            jax.ShapeDtypeStruct((2, pairs, inner), bf16),
+            jax.ShapeDtypeStruct((2, pairs, half), bf16),
+        ),
+        in_specs=[everywhere, everywhere, everywhere, vmem, vmem, everywhere],
+        out_specs=(vmem, vmem, vmem),
+        scratch_shapes=[
+            pltpu.VMEM((CHUNKS, nz, tokens, width), bf16),
+            pltpu.VMEM((nz,) + meta.shape, jnp.float32),
+            pltpu.VMEM((CHUNKS, 2, spots, slots, width), bf16),
+            pltpu.VMEM((spots, slots, features), bf16),
+            pltpu.VMEM((2, pairs, features), bf16),
+            pltpu.VMEM((2, inner, half), bf16),
+            pltpu.VMEM((2, pairs, inner), bf16),
+            pltpu.VMEM((pairs, inner), bf16),
+            semaphores((CHUNKS,)),
+            semaphores((CHUNKS,)),
+            semaphores((2,)),
+            semaphores((CHUNKS,)),
+            semaphores((CHUNKS,)),
+            semaphores((CHUNKS,)),
+            semaphores((CHUNKS,)),
+            semaphores((3,)),
+            semaphores((3,)),
+            semaphores((CHUNKS + 3,)),
+            semaphores((CHUNKS,)),
+        ],
+        compiler_params=pltpu.CompilerParams(
+            collective_id=1, has_side_effects=True, vmem_limit_bytes=48 * 2**20
+        ),
+        name="route",
+    )(meta, dy, inputs, gate, up, down)
 
 
 def orthogonal_factor(kernel_matrix, rows):
@@ -244,47 +428,19 @@
     up_weight,
     new_owner,
 ):
-    copy_index = lax.axis_index("rep")
+    first = lax.axis_index("rep") == 0
     experts = lax.axis_size("ep")
-    capacity = saved_inputs.shape[3]
     tokens, width = dy.shape
+    top = expert_ids.shape[1]
     inner = saved_gate.shape[4]
     half = width // 2
-    first = copy_index == 0
-
+    keyed = (expert_ids * 2 + copy_choice).astype(jnp.float32)
+    meta = jnp.concatenate([keyed, probs, jnp.zeros((tokens, 128 - 2 * top), jnp.float32)], axis=1)
+    kernel_matrix, rows, columns = route(
+        meta, dy, saved_inputs.reshape(-1, width), saved_gate[0, 0], saved_up[0, 0], down_weight[0], top
+    )
+    factor_rows, columns = rows.reshape(-1, inner), columns.reshape(-1, half)
     expert = jnp.arange(experts, dtype=jnp.int32)
-    hits = (expert_ids[:, :, None] == expert) & (copy_choice == copy_index)[:, :, None]
-    chosen = jnp.any(hits, axis=1)
-    weight = jnp.sum(jnp.where(hits, probs[:, :, None], 0.0), axis=1)
-    before = jnp.tril(jnp.ones((tokens, tokens), jnp.bfloat16), -1)
-    position = jnp.dot(before, chosen.astype(jnp.bfloat16), preferred_element_type=jnp.float32)
-    slot = jnp.arange(capacity, dtype=jnp.float32)
-    select = chosen[:, :, None] & (position[:, :, None] == slot)
-    scale = jnp.sum(jnp.where(select, weight[:, :, None], 0.0), axis=0)
-    rows = lax.dot_general(
-        select.astype(jnp.bfloat16), dy, (((0,), (0,)), ((), ())), preferred_element_type=jnp.float32
-    )
-    outgoing = (scale[:, :, None] * rows).astype(jnp.bfloat16)
-    routed = exchange(outgoing).reshape(experts * capacity, width)
-
-    def ordered(own, other, axis):
-        return jnp.where(first, jnp.concatenate([own, other], axis), jnp.concatenate([other, own], axis))
-
-    down = down_weight[0]
-    hidden_grad = dot(routed, ordered(down, from_partner(down), 1), ((1,), (1,))) / math.sqrt(inner)
-    gate_value = saved_gate.reshape(-1, inner).astype(jnp.float32)
-    up_value = saved_up.reshape(-1, inner).astype(jnp.float32)
-    sigmoid = jax.nn.sigmoid(gate_value)
-    gate_rows = (hidden_grad * up_value * sigmoid * (1.0 + gate_value * (1.0 - sigmoid))).astype(jnp.bfloat16)
-    up_rows = (hidden_grad * gate_value * sigmoid).astype(jnp.bfloat16)
-    own_rows = jnp.where(first, gate_rows, up_rows)
-    other_rows = from_partner(jnp.where(first, up_rows, gate_rows))
-    factor_rows = ordered(own_rows, other_rows, 0)
-
-    inputs = saved_inputs.reshape(-1, width)
-    all_inputs = ordered(inputs, from_partner(inputs), 0)
-    kernel_matrix = dot(all_inputs, all_inputs, ((1,), (1,)))
-    columns = jnp.where(first, all_inputs[:, :half], all_inputs[:, half:])
     inverse = jnp.sum(
         jnp.where(new_owner[:, None] == expert[None, :], expert[:, None], 0), axis=0, dtype=jnp.int32
     )

time: 219 us -> 199 us (0.909)
  local copies, waits for them, and re-layouts: 11 us -> 3.84 us
  starting transfers between devices: 5.47 us -> 0 us
  matrix products: 5.3 us -> 0 us
    ppermute x3 -> x0, starting transfers between devices: 5.47 us -> none  [from_partner(): return lax.ppermute(block, 'rep', [(0, 1), (1, 0)])]
    dot_general x4 -> x0, matrix products: 5.3 us -> none  [the longest x2 4.63 us: dot(): lax.dot_general(a, b, (dims, ((), ())), preferred_element_type=jnp.float32)]
    pallas_call x1, Pallas kernels: 154 us -> 150 us  [move(): pl.pallas_call(functools.partial(move_kernel, n, factor), out_shape=(shap...]
    pallas_call x1, Pallas kernels: 37.8 us -> 42.2 us  [route(): pl.pallas_call(functools.partial(route_kernel, top), out_shape=(jax.Shape...]
    convert_element_type x2 -> x0, local copies, waits for them, and re-layouts: 3.97 us -> none  [the longest x1 1.99 us: shards(): up_value = saved_up.reshape(-1, inner).astype(jnp.float32)]
  transfers between devices with their start and end apart: 3 -> 0, of which waited for: 1 -> 0; matrix products, arithmetic and copies ran while one was open for 6% -> 0% of each run, Pallas kernels for 17% -> 0%
where the time goes in v1:
time: 199 us
  Pallas kernels  192 us (96%)
  local copies, waits for them, and re-layouts  3.84 us (2%)
  other arithmetic  2.78 us (1%)
    pallas_call x1, Pallas kernels, move(): pl.pallas_call(functools.partial(move_kernel, n, factor), out_shape=(shap...  150 us
    pallas_call x1, Pallas kernels, route(): pl.pallas_call(functools.partial(route_kernel, top), out_shape=(jax.Shape...  42.2 us

profile of v1, /device:TPU:1, one launch (start us, length us, event | category | flops | bytes accessed | tf_op | source)
XLA Modules:
  0.0 199.0 jit_solution(11005896796274427728)
XLA Ops:
  0.6 0.0 copy-start.1
  0.6 0.0 copy-start
  0.7 0.0 copy-start.2
  0.7 0.8 select_reduce_fusion.inverse
  1.5 0.1 pad.2.clone
  1.6 0.8 copy.22
  2.3 0.8 copy.19
  3.1 0.8 copy.21
  3.9 0.1 maximum_maximum_fusion.meta_ref
  4.0 1.5 reshape.20.x_ref
  5.4 0.0 copy-done.1
  5.4 0.0 copy-done
  5.4 0.0 copy-done.2
  5.5 42.2 %route.1 = (f32[512,512]{1,0:T(8,128)S(1)}, bf16[2,256,768]{2,1,0:T(8,128)(2,1)S(1)}, bf16[2,256,1024]{2,1,0:T(8,128)(2,1)S(1)}) custom-call(f32[32,128]{1,0:T(8,128)S(1)} %maximum_maximum_fusion.meta_ref, bf16[32,2048]{1,0:T(8,128)(2,1)S(1)} %copy-done.2, bf16[256,2048]{1,0:T(8,128)(2,1)S(1)} %reshape.20.x_ref, bf16[128,2,768]{2,1,0:T(2,128)(2,1)S(1)} %bitcast.13, ...), custom_call_target="tpu_custom_call" | custom-call | tf_op jit(solution)/shard_map/route/pallas_call | solution.py:234
  47.6 149.5 %move.1 = (bf16[128,8,768]{2,1,0:T(8,128)(2,1)S(1)}, bf16[128,8,768]{2,1,0:T(8,128)(2,1)S(1)}) custom-call(s32[128]{0:T(128)S(1)} %select_reduce_fusion.inverse, f32[512,512]{1,0:T(8,128)S(1)} %get-tuple-element.7.k_ref, bf16[512,768]{1,0:T(8,128)(2,1)S(1)} %bitcast.12, bf16[512,1024]{1,0:T(8,128)(2,1)S(1)} %bitcast.11, bf16[1024,768]{1,0:T(8,128)(2,1)} %bitcast.16, ...), custom_call_target="tpu_custom_call" | custom-call | tf_op jit(solution)/shard_map/move/pallas_call | solution.py:394
  197.1 1.9 select_bitcast_fusion
  (2 shorter events, 0.0 us)
Async XLA Ops:
  0.6 4.8 %copy-start.1 = (bf16[1,1,128,2,768]{4,3,2,1,0:T(2,128)(2,1)S(1)}, bf16[1,1,128,2,768]{4,3,2,1,0:T(2,128)(2,1)}, u32[]{:S(2)}) copy-start(bf16[1,1,128,2,768]{4,3,2,1,0:T(2,128)(2,1)} %param.17) | copy-start | bytes 1179652
  0.6 4.8 %copy-start = (bf16[1,1,128,2,768]{4,3,2,1,0:T(2,128)(2,1)S(1)}, bf16[1,1,128,2,768]{4,3,2,1,0:T(2,128)(2,1)}, u32[]{:S(2)}) copy-start(bf16[1,1,128,2,768]{4,3,2,1,0:T(2,128)(2,1)} %param.16) | copy-start | bytes 1179652
  0.7 4.8 %copy-start.2 = (bf16[32,2048]{1,0:T(8,128)(2,1)S(1)}, bf16[32,2048]{1,0:T(8,128)(2,1)}, u32[]{:S(2)}) copy-start(bf16[32,2048]{1,0:T(8,128)(2,1)} %dy_ref.1) | copy-start | bytes 393220

commit v2 on v1

--- a/solution.py
+++ b/solution.py
@@ -31,7 +31,7 @@
     return lax.dot_general(a, b, (dims, ((), ())), preferred_element_type=jnp.float32)
 
 
-CHUNKS = 2
+CHUNKS = 4
 
 
 def shift_of(size):
@@ -39,7 +39,7 @@
     return size.bit_length() - 1
 
 
-def selection(key_columns, plane, top, sources, tokens, spots, capacity):
+def selection(table, plane, top, sources, tokens, spots, capacity):
     count = sources * tokens
     lanes = 2 * spots * sources * capacity
     lane = lax.broadcasted_iota(jnp.int32, (1, lanes), 1)
@@ -48,13 +48,20 @@
     spot = (lane >> shift_of(capacity * sources)) & (spots - 1)
     copy = lane >> shift_of(capacity * sources * spots)
     wanted = (((spot * sources + plane) * 2) + copy).astype(jnp.float32)
-    here = (lax.broadcasted_iota(jnp.int32, (count, 1), 0) >> shift_of(tokens)) == source
-    taken = jnp.zeros((count, lanes), jnp.float32)
-    weight = jnp.zeros((count, lanes), jnp.float32)
-    for k in range(top):
-        hit = (key_columns[:, k : k + 1] == wanted) & here
-        taken = jnp.where(hit, 1.0, taken)
-        weight = jnp.where(hit, key_columns[:, top + k : top + k + 1], weight)
+    blocks, weights = [], []
+    for z in range(sources):
+        aim = jnp.where(source == z, wanted, -1.0)
+        block = jnp.zeros((tokens, lanes), jnp.float32)
+        weight = jnp.zeros((tokens, lanes), jnp.float32)
+        for k in range(top):
+            at = z * 2 * top + k
+            hit = table[:, at : at + 1] == aim
+            block = jnp.where(hit, 1.0, block)
+            weight = jnp.where(hit, table[:, at + top : at + top + 1], weight)
+        blocks.append(block)
+        weights.append(weight)
+    taken = jnp.concatenate(blocks, axis=0)
+    weight = jnp.concatenate(weights, axis=0)
     row = lax.broadcasted_iota(jnp.int32, (count, count), 0)
     column = lax.broadcasted_iota(jnp.int32, (count, count), 1)
     before = jnp.where(row > column, 1.0, 0.0).astype(jnp.bfloat16)
@@ -78,8 +85,8 @@
 
 
 def route_kernel(
-    top, meta_ref, dy_ref, x_ref, g_ref, u_ref, down_ref, k_out, r_out, x_out,
-    line, keys, sent, routed, inputs, down, rows, other,
+    top, ids_ref, copy_ref, probs_ref, owner_ref, dy_ref, x_ref, g_ref, u_ref, down_ref, k_out, r_out, x_out, inverse_out,
+    line, meta, gates, keys, sent, routed, raw, inputs, down, rows, other,
     line_send, line_recv, keys_sem, plane_send, plane_recv, near_send, near_recv, pair_send, pair_recv,
     own_sem, piece_sem,
 ):
@@ -96,6 +103,10 @@
     def above(k):
         return {"ep": shifted(me, k)}
 
+    count = ids_ref.shape[1]
+    keyed = (ids_ref[...] * 2 + copy_ref[...]).astype(jnp.float32)
+    packed = jnp.concatenate([keyed, probs_ref[...]], axis=0)
+    meta[...] = jnp.concatenate([packed, jnp.zeros((2 * top, 128 - count), jnp.float32)], axis=1)
     barrier = pltpu.get_barrier_semaphore()
 
     def greet_line(k, carry):
@@ -117,15 +128,17 @@
         return pl.ds(pl.multiple_of(core * half + chunk * width, width), width)
 
     own = [pltpu.make_async_copy(dy_ref.at[:, columns(h)], line.at[h, z], own_sem.at[h]) for h in range(CHUNKS)]
-    own.append(pltpu.make_async_copy(meta_ref, keys.at[z], own_sem.at[CHUNKS]))
-    own.append(pltpu.make_async_copy(x_ref, inputs.at[core], own_sem.at[CHUNKS + 1]))
+    own.append(pltpu.make_async_copy(meta, keys.at[z], own_sem.at[CHUNKS]))
+    own.append(pltpu.make_async_copy(x_ref, raw.at[core], own_sem.at[CHUNKS + 1]))
     own.append(pltpu.make_async_copy(down_ref, down.at[core], own_sem.at[CHUNKS + 2]))
+    own.append(pltpu.make_async_copy(g_ref, gates.at[0], own_sem.at[CHUNKS + 3]))
+    own.append(pltpu.make_async_copy(u_ref, gates.at[1], own_sem.at[CHUNKS + 4]))
     for copy in own:
         copy.start()
     pl.semaphore_wait(barrier, nz + 2 * (spots - 1))
 
     def send_keys(k, carry):
-        remote(meta_ref, keys.at[z], keys_sem.at[0], keys_sem.at[1], above(k)).start()
+        remote(meta, keys.at[z], keys_sem.at[0], keys_sem.at[1], above(k)).start()
         return carry
 
     lax.fori_loop(1, nz, send_keys, 0)
@@ -137,7 +150,7 @@
 
         lax.fori_loop(1, nz, send_line, 0)
     swaps = [
-        remote(x_ref, inputs.at[core], pair_send.at[0], pair_recv.at[0], partner),
+        remote(x_ref, raw.at[core], pair_send.at[0], pair_recv.at[0], partner),
         remote(down_ref, down.at[core], pair_send.at[1], pair_recv.at[1], partner),
     ]
     for swap in swaps:
@@ -147,8 +160,9 @@
     all_keys = remote(keys.at[others], keys.at[others], keys_sem.at[0], keys_sem.at[1], above(1))
     all_keys.wait_recv()
     own[CHUNKS].wait()
+    table = keys[...].reshape(nz * 2 * top, 128).T
     choose, scale = selection(
-        keys[...].reshape(nz * tokens, keys.shape[2]), z, top, nz, tokens, spots, capacity
+        table[:count], z, top, nz, tokens, spots, capacity
     )
     scale = jnp.concatenate([scale] * (width // scale.shape[1]), axis=1)
     for h in range(CHUNKS):
@@ -177,25 +191,36 @@
     own[CHUNKS + 1].wait()
     swaps[0].wait_recv()
     copies, pairs, features = inputs.shape
+    for c in range(2):
+        inputs[c] = raw[c].astype(jnp.float32).reshape(pairs, features).astype(jnp.bfloat16)
     everything = inputs[...].reshape(copies * pairs, features)
     k_out[...] = dot(everything, everything, ((1,), (1,)))
     for c in range(2):
         x_out[c] = inputs[c, :, pl.ds(pl.multiple_of(core * half, half), half)]
-    gate_value = g_ref[...].astype(jnp.float32).reshape(pairs, g_ref.shape[-1])
-    up_value = u_ref[...].astype(jnp.float32).reshape(pairs, u_ref.shape[-1])
+    own[CHUNKS + 3].wait()
+    own[CHUNKS + 4].wait()
+    gate_value = gates[0].astype(jnp.float32).reshape(pairs, g_ref.shape[-1])
+    up_value = gates[1].astype(jnp.float32).reshape(pairs, u_ref.shape[-1])
+    experts = owner_ref.shape[1]
+    low = lax.broadcasted_iota(jnp.int32, (experts, experts), 0)
+    wide = lax.broadcasted_iota(jnp.int32, (experts, experts), 1).astype(jnp.float32)
+    held = jnp.sum(jnp.where(owner_ref[...] == low, wide, 0.0), axis=1, keepdims=True)
+    inverse_out[...] = jnp.broadcast_to(held, (experts, experts)).T[:1].astype(jnp.int32)
     own[CHUNKS + 2].wait()
     swaps[1].wait_recv()
     near = pl.ds(0, spots - 1)
+    hidden = None
     for h in range(CHUNKS):
         pltpu.make_async_copy(sent.at[h, core, spot], routed.at[spot, :, columns(h)], piece_sem.at[h]).wait()
         remote(
             sent.at[h, 1 - core, spot], routed.at[spot, :, columns(h)], near_send.at[h], near_recv.at[h], partner
         ).wait_recv()
-        both = routed.at[near, :, pl.ds(h * 2 * width, 2 * width)]
+        both = sent.at[h, :, near]
         remote(both, both, plane_send.at[h], plane_recv.at[h], partner).wait_recv()
-
-    arrived = routed[...].reshape(pairs, features)
-    hidden = dot(arrived[:, :half], down[0], ((1,), (1,))) + dot(arrived[:, half:], down[1], ((1,), (1,)))
+        for c in range(2):
+            here = routed[:, :, pl.ds(c * half + h * width, width)].reshape(pairs, width)
+            term = dot(here, down[c, :, pl.ds(h * width, width)], ((1,), (1,)))
+            hidden = term if hidden is None else hidden + term
     hidden = hidden / math.sqrt(hidden.shape[1])
     sigmoid = jax.nn.sigmoid(gate_value)
     gate_rows = hidden * up_value * sigmoid * (1.0 + gate_value * (1.0 - sigmoid))
@@ -221,14 +246,15 @@
     r_out[...] = rows[...]
 
 
-def route(meta, dy, inputs, gate, up, down, top):
-    pairs, features = inputs.shape
+def route(ids, copies, probs, owner, dy, inputs, gate, up, down):
+    top = ids.shape[0]
+    pairs, features = inputs.shape[0] * inputs.shape[1], inputs.shape[2]
     inner, half = down.shape
     tokens = dy.shape[0]
     nz, spots = GRID[2], GRID[0] * GRID[1]
     slots = pairs // spots
     width = half // CHUNKS
-    everywhere, vmem = pl.BlockSpec(memory_space=pl.ANY), pl.BlockSpec(memory_space=pltpu.VMEM)
+    everywhere, vmem = pl.BlockSpec(memory_space=pltpu.HBM), pl.BlockSpec(memory_space=pltpu.VMEM)
     bf16 = jnp.bfloat16
     semaphores = pltpu.SemaphoreType.DMA
     return pl.pallas_call(
@@ -237,14 +263,18 @@
             jax.ShapeDtypeStruct((2 * pairs, 2 * pairs), jnp.float32),
             jax.ShapeDtypeStruct((2, pairs, inner), bf16),
             jax.ShapeDtypeStruct((2, pairs, half), bf16),
+            jax.ShapeDtypeStruct(owner.shape, jnp.int32),
         ),
-        in_specs=[everywhere, everywhere, everywhere, vmem, vmem, everywhere],
-        out_specs=(vmem, vmem, vmem),
+        in_specs=[vmem] * 4 + [everywhere] * 5,
+        out_specs=(vmem, vmem, vmem, vmem),
         scratch_shapes=[
             pltpu.VMEM((CHUNKS, nz, tokens, width), bf16),
-            pltpu.VMEM((nz,) + meta.shape, jnp.float32),
+            pltpu.VMEM((2 * top, 128), jnp.float32),
+            pltpu.VMEM((2,) + gate.shape, bf16),
+            pltpu.VMEM((nz, 2 * top, 128), jnp.float32),
             pltpu.VMEM((CHUNKS, 2, spots, slots, width), bf16),
             pltpu.VMEM((spots, slots, features), bf16),
+            pltpu.VMEM((2,) + inputs.shape, bf16),
             pltpu.VMEM((2, pairs, features), bf16),
             pltpu.VMEM((2, inner, half), bf16),
             pltpu.VMEM((2, pairs, inner), bf16),
@@ -258,31 +288,31 @@
             semaphores((CHUNKS,)),
             semaphores((3,)),
             semaphores((3,)),
-            semaphores((CHUNKS + 3,)),
+            semaphores((CHUNKS + 5,)),
             semaphores((CHUNKS,)),
         ],
         compiler_params=pltpu.CompilerParams(
             collective_id=1, has_side_effects=True, vmem_limit_bytes=48 * 2**20
         ),
         name="route",
-    )(meta, dy, inputs, gate, up, down)
+    )(ids, copies, probs, owner, dy, inputs, gate, up, down)
 
 
 def orthogonal_factor(kernel_matrix, rows):
     high = kernel_matrix.astype(jnp.bfloat16)
     low = (kernel_matrix - high.astype(jnp.float32)).astype(jnp.bfloat16)
-    product = dot(high, rows, ((1,), (0,))) + dot(low, rows, ((1,), (0,)))
-    total = jnp.sqrt(jnp.maximum(jnp.sum(rows.astype(jnp.float32) * product), 0.0))
-    scale = 1.0 / (total + epsilon)
-    product = product * (scale * scale)
+    scale = None
     for repeat in range(ITERS):
-        if repeat:
-            product = dot(high, rows, ((1,), (0,))) + dot(low, rows, ((1,), (0,)))
-        gram = dot(rows, product.astype(jnp.bfloat16), ((0,), (0,)))
+        square = dot(rows, rows, ((1,), (1,)))
+        if not repeat:
+            total = jnp.sqrt(jnp.maximum(jnp.sum(square * kernel_matrix), 0.0))
+            scale = 1.0 / (total + epsilon)
+            square = square * (scale * scale)
+        square = square.astype(jnp.bfloat16)
+        gram = dot(square, high, ((1,), (0,))) + dot(square, low, ((1,), (0,)))
         half = gram.astype(jnp.bfloat16)
-        square = dot(half, half, ((1,), (0,)))
-        poly = (quintic_second * gram + quintic_third * square).astype(jnp.bfloat16)
-        mixed = quintic_first * rows.astype(jnp.float32) + dot(rows, poly, ((1,), (0,)))
+        poly = quintic_second * gram + quintic_third * dot(half, half, ((1,), (0,)))
+        mixed = quintic_first * rows.astype(jnp.float32) + dot(poly.astype(jnp.bfloat16), rows, ((1,), (0,)))
         if not repeat:
             mixed = mixed * scale
         rows = mixed.astype(jnp.bfloat16)
@@ -430,20 +460,14 @@
 ):
     first = lax.axis_index("rep") == 0
     experts = lax.axis_size("ep")
-    tokens, width = dy.shape
-    top = expert_ids.shape[1]
+    width = dy.shape[1]
     inner = saved_gate.shape[4]
     half = width // 2
-    keyed = (expert_ids * 2 + copy_choice).astype(jnp.float32)
-    meta = jnp.concatenate([keyed, probs, jnp.zeros((tokens, 128 - 2 * top), jnp.float32)], axis=1)
-    kernel_matrix, rows, columns = route(
-        meta, dy, saved_inputs.reshape(-1, width), saved_gate[0, 0], saved_up[0, 0], down_weight[0], top
-    )
-    factor_rows, columns = rows.reshape(-1, inner), columns.reshape(-1, half)
-    expert = jnp.arange(experts, dtype=jnp.int32)
-    inverse = jnp.sum(
-        jnp.where(new_owner[:, None] == expert[None, :], expert[:, None], 0), axis=0, dtype=jnp.int32
-    )
+    kernel_matrix, rows, columns, inverse = route(
+        expert_ids.T, copy_choice.T, probs.T, new_owner.reshape(1, experts), dy, saved_inputs[0, 0],
+        saved_gate[0, 0], saved_up[0, 0], down_weight[0],
+    )
+    factor_rows, columns, inverse = rows.reshape(-1, inner), columns.reshape(-1, half), inverse.reshape(experts)
     own, other = move(
         experts, step_scale * math.sqrt(width), inverse, kernel_matrix, factor_rows, columns, gate_weight[0], up_weight[0]
     )

time: 199 us -> 195 us (0.980)
  Pallas kernels: 192 us -> 185 us
  local copies, waits for them, and re-layouts: 3.84 us -> 6.83 us
    pallas_call x1, Pallas kernels: 42.2 us -> 36.1 us  [route(): pl.pallas_call(functools.partial(route_kernel, top), out_shape=(jax.Shape...]
    unnamed x9 -> x16, local copies, waits for them, and re-layouts: 2.3 us -> 6.83 us
where the time goes in v2:
time: 195 us; the launch traced here: 194 us
  Pallas kernels  185 us (95%)
  local copies, waits for them, and re-layouts  6.83 us (4%)
    pallas_call x1, Pallas kernels, move(): pl.pallas_call(functools.partial(move_kernel, n, factor), out_shape=(shap...  149 us
    pallas_call x1, Pallas kernels, route(): pl.pallas_call(functools.partial(route_kernel, top), out_shape=(jax.Shape...  36.1 us
    unnamed x16, local copies, waits for them, and re-layouts  6.83 us

profile of v2, /device:TPU:1, one launch (start us, length us, event | category | flops | bytes accessed | tf_op | source)
XLA Modules:
  0.0 194.4 jit_solution(11920445485970392214)
XLA Ops:
  0.6 0.0 copy-start
  0.6 1.2 copy-done
  1.9 0.0 copy-start.1
  1.9 1.0 copy-done.1
  2.9 0.0 copy-start.2
  2.9 1.0 copy-done.2
  3.9 0.0 copy-start.3
  3.9 0.9 copy-done.3
  4.8 0.0 copy-start.4
  4.8 0.7 copy-done.4
  5.4 0.0 copy-start.5
  5.5 0.7 copy-done.5
  6.1 0.0 copy-start.6
  6.1 0.7 copy-done.6
  6.8 0.0 copy-start.7
  6.8 0.7 copy-done.7
  7.5 36.1 %route.1 = (f32[512,512]{1,0:T(8,128)S(1)}, bf16[2,256,768]{2,1,0:T(8,128)(2,1)S(1)}, bf16[2,256,1024]{2,1,0:T(8,128)(2,1)S(1)}, s32[1,128]{1,0:T(1,128)S(1)}) custom-call(s32[8,32]{1,0:T(8,128)S(1)} %bitcast.22, s32[8,32]{1,0:T(8,128)S(1)} %bitcast.23, f32[8,32]{1,0:T(8,128)S(1)} %bitcast.24, s32[1,128]{1,0:T(1,128)S(1)} %bitcast.25, ...), custom_call_target="tpu_custom_call" | custom-call | tf_op jit(solution)/shard_map/route/pallas_call | solution.py:260
  43.6 148.9 %move.1 = (bf16[128,8,768]{2,1,0:T(8,128)(2,1)S(1)}, bf16[128,8,768]{2,1,0:T(8,128)(2,1)S(1)}) custom-call(s32[128]{0:T(128)S(1)} %bitcast.26, f32[512,512]{1,0:T(8,128)S(1)} %get-tuple-element.9.k_ref, bf16[512,768]{1,0:T(8,128)(2,1)S(1)} %bitcast.19, bf16[512,1024]{1,0:T(8,128)(2,1)S(1)} %bitcast.18, bf16[1024,768]{1,0:T(8,128)(2,1)} %bitcast.28, ...), custom_call_target="tpu_custom_call" | custom-call | tf_op jit(solution)/shard_map/move/pallas_call | solution.py:424
  192.5 1.9 select_bitcast_fusion
Async XLA Ops:
  0.6 1.2 copy-start
  1.9 1.0 copy-start.1
  2.9 1.0 copy-start.2
  3.9 0.9 copy-start.3
  4.8 0.7 copy-start.4
  5.4 0.7 copy-start.5
  6.1 0.7 copy-start.6
  6.8 0.7 copy-start.7

commit v3 on v2

--- a/solution.py
+++ b/solution.py
@@ -86,9 +86,10 @@
 
 def route_kernel(
     top, ids_ref, copy_ref, probs_ref, owner_ref, dy_ref, x_ref, g_ref, u_ref, down_ref, k_out, r_out, x_out, inverse_out,
+    ids, copies_of, probs, owners, products, slices, spread_of,
     line, meta, gates, keys, sent, routed, raw, inputs, down, rows, other,
     line_send, line_recv, keys_sem, plane_send, plane_recv, near_send, near_recv, pair_send, pair_recv,
-    own_sem, piece_sem,
+    own_sem, piece_sem, small_sem, out_sem,
 ):
     me = lax.axis_index("ep")
     core = lax.axis_index("rep")
@@ -104,9 +105,14 @@
         return {"ep": shifted(me, k)}
 
     count = ids_ref.shape[1]
-    keyed = (ids_ref[...] * 2 + copy_ref[...]).astype(jnp.float32)
-    packed = jnp.concatenate([keyed, probs_ref[...]], axis=0)
-    meta[...] = jnp.concatenate([packed, jnp.zeros((2 * top, 128 - count), jnp.float32)], axis=1)
+    small = [
+        pltpu.make_async_copy(src, dst, small_sem.at[i])
+        for i, (src, dst) in enumerate(
+            ((ids_ref, ids), (copy_ref, copies_of), (probs_ref, probs), (owner_ref, owners))
+        )
+    ]
+    for copy in small:
+        copy.start()
     barrier = pltpu.get_barrier_semaphore()
 
     def greet_line(k, carry):
@@ -133,6 +139,11 @@
     own.append(pltpu.make_async_copy(down_ref, down.at[core], own_sem.at[CHUNKS + 2]))
     own.append(pltpu.make_async_copy(g_ref, gates.at[0], own_sem.at[CHUNKS + 3]))
     own.append(pltpu.make_async_copy(u_ref, gates.at[1], own_sem.at[CHUNKS + 4]))
+    for copy in small[:3]:
+        copy.wait()
+    keyed = (ids[...] * 2 + copies_of[...]).astype(jnp.float32)
+    packed = jnp.concatenate([keyed, probs[...]], axis=0)
+    meta[...] = jnp.concatenate([packed, jnp.zeros((2 * top, 128 - count), jnp.float32)], axis=1)
     for copy in own:
         copy.start()
     pl.semaphore_wait(barrier, nz + 2 * (spots - 1))
@@ -141,7 +152,6 @@
         remote(meta, keys.at[z], keys_sem.at[0], keys_sem.at[1], above(k)).start()
         return carry
 
-    lax.fori_loop(1, nz, send_keys, 0)
     for h in range(CHUNKS):
 
         def send_line(k, carry, h=h):
@@ -149,6 +159,8 @@
             return carry
 
         lax.fori_loop(1, nz, send_line, 0)
+        if not h:
+            lax.fori_loop(1, nz, send_keys, 0)
     swaps = [
         remote(x_ref, raw.at[core], pair_send.at[0], pair_recv.at[0], partner),
         remote(down_ref, down.at[core], pair_send.at[1], pair_recv.at[1], partner),
@@ -194,9 +206,8 @@
     for c in range(2):
         inputs[c] = raw[c].astype(jnp.float32).reshape(pairs, features).astype(jnp.bfloat16)
     everything = inputs[...].reshape(copies * pairs, features)
-    k_out[...] = dot(everything, everything, ((1,), (1,)))
-    for c in range(2):
-        x_out[c] = inputs[c, :, pl.ds(pl.multiple_of(core * half, half), half)]
+    products[...] = dot(everything, everything, ((1,), (1,)))
+    slices[...] = inputs[:, :, pl.ds(pl.multiple_of(core * half, half), half)]
     own[CHUNKS + 3].wait()
     own[CHUNKS + 4].wait()
     gate_value = gates[0].astype(jnp.float32).reshape(pairs, g_ref.shape[-1])
@@ -204,8 +215,17 @@
     experts = owner_ref.shape[1]
     low = lax.broadcasted_iota(jnp.int32, (experts, experts), 0)
     wide = lax.broadcasted_iota(jnp.int32, (experts, experts), 1).astype(jnp.float32)
-    held = jnp.sum(jnp.where(owner_ref[...] == low, wide, 0.0), axis=1, keepdims=True)
-    inverse_out[...] = jnp.broadcast_to(held, (experts, experts)).T[:1].astype(jnp.int32)
+    small[3].wait()
+    held = jnp.sum(jnp.where(owners[...] == low, wide, 0.0), axis=1, keepdims=True)
+    spread_of[...] = jnp.broadcast_to(held, (experts, experts)).T[:1].astype(jnp.int32)
+    outgoing = [
+        pltpu.make_async_copy(src, dst, out_sem.at[i])
+        for i, (src, dst) in enumerate(
+            ((products, k_out), (slices, x_out), (spread_of, inverse_out), (rows, r_out))
+        )
+    ]
+    for copy in outgoing[:3]:
+        copy.start()
     own[CHUNKS + 2].wait()
     swaps[1].wait_recv()
     near = pl.ds(0, spots - 1)
@@ -231,6 +251,8 @@
     last = remote(other, rows.at[core], pair_send.at[2], pair_recv.at[2], partner)
     last.start()
 
+    last.wait_recv()
+    outgoing[3].start()
     all_keys.wait_send()
     for swap in swaps:
         swap.wait_send()
@@ -242,8 +264,8 @@
         both = sent.at[h, :, near]
         remote(both, both, plane_send.at[h], plane_recv.at[h], partner).wait_send()
     last.wait_send()
-    last.wait_recv()
-    r_out[...] = rows[...]
+    for copy in outgoing:
+        copy.wait()
 
 
 def route(ids, copies, probs, owner, dy, inputs, gate, up, down):
@@ -254,7 +276,7 @@
     nz, spots = GRID[2], GRID[0] * GRID[1]
     slots = pairs // spots
     width = half // CHUNKS
-    everywhere, vmem = pl.BlockSpec(memory_space=pltpu.HBM), pl.BlockSpec(memory_space=pltpu.VMEM)
+    everywhere = pl.BlockSpec(memory_space=pl.ANY)
     bf16 = jnp.bfloat16
     semaphores = pltpu.SemaphoreType.DMA
     return pl.pallas_call(
@@ -265,9 +287,16 @@
             jax.ShapeDtypeStruct((2, pairs, half), bf16),
             jax.ShapeDtypeStruct(owner.shape, jnp.int32),
         ),
-        in_specs=[vmem] * 4 + [everywhere] * 5,
-        out_specs=(vmem, vmem, vmem, vmem),
+        in_specs=[everywhere] * 9,
+        out_specs=(everywhere,) * 4,
         scratch_shapes=[
+            pltpu.VMEM(ids.shape, jnp.int32),
+            pltpu.VMEM(ids.shape, jnp.int32),
+            pltpu.VMEM(ids.shape, jnp.float32),
+            pltpu.VMEM(owner.shape, jnp.int32),
+            pltpu.VMEM((2 * pairs, 2 * pairs), jnp.float32),
+            pltpu.VMEM((2, pairs, half), bf16),
+            pltpu.VMEM(owner.shape, jnp.int32),
             pltpu.VMEM((CHUNKS, nz, tokens, width), bf16),
             pltpu.VMEM((2 * top, 128), jnp.float32),
             pltpu.VMEM((2,) + gate.shape, bf16),
@@ -290,9 +319,11 @@
             semaphores((3,)),
             semaphores((CHUNKS + 5,)),
             semaphores((CHUNKS,)),
+            semaphores((4,)),
+            semaphores((4,)),
         ],
         compiler_params=pltpu.CompilerParams(
-            collective_id=1, has_side_effects=True, vmem_limit_bytes=48 * 2**20
+            collective_id=1, has_side_effects=True, vmem_limit_bytes=63 * 2**20
         ),
         name="route",
     )(ids, copies, probs, owner, dy, inputs, gate, up, down)
@@ -320,8 +351,8 @@
 
 
 def move_kernel(
-    n, factor, inverse, k_ref, r_ref, x_ref, gate_ref, up_ref, own_out, other_out,
-    weights, factors, made0, made1, held0, held1, ready0, ready1, load, send, recv, local, swap,
+    n, factor, inverse_ref, k_ref, r_ref, x_ref, gate_ref, up_ref, own_out, other_out,
+    inverse, products, begin, columns, weights, factors, made0, made1, held0, held1, ready0, ready1, load, send, recv, local, swap, fetch,
 ):
     me = lax.axis_index("ep")
     core = lax.axis_index("rep")
@@ -333,6 +364,14 @@
     rest = pl.ds(0, n - 1)
     partner = {"rep": 1 - core}
 
+    fetches = [
+        pltpu.make_async_copy(src, dst, fetch.at[i])
+        for i, (src, dst) in enumerate(
+            ((k_ref, products), (r_ref, begin), (x_ref, columns), (inverse_ref, inverse))
+        )
+    ]
+    for copy in fetches:
+        copy.start()
     barrier = pltpu.get_barrier_semaphore()
 
     def say(k, carry):
@@ -348,13 +387,17 @@
             for q in range(2):
                 pltpu.make_async_copy(refs[q], weights.at[q], load.at[q]).start()
 
-    factors[0] = orthogonal_factor(k_ref[...], r_ref[...])
+    fetches[0].wait()
+    fetches[1].wait()
+    factors[0] = orthogonal_factor(products[...], begin[...])
     pl.semaphore_wait(barrier, n)
     trade = pltpu.make_async_remote_copy(
         src_ref=factors.at[0], dst_ref=factors.at[1], send_sem=swap.at[0], recv_sem=swap.at[1],
         device_id=partner, device_id_type=MESH,
     )
     trade.start()
+    fetches[2].wait()
+    fetches[3].wait()
 
     for q in range(2):
         pltpu.make_async_copy(gate_ref, weights.at[q], load.at[q]).wait()
@@ -372,7 +415,7 @@
         def produce(dy, carry, q=q):
             y = lax.rem(me // group + dy, ny)
             rows = pl.ds(pl.multiple_of(y * block, block), block)
-            ortho = dot(x_ref[:, rows], factors[q], ((0,), (0,)))
+            ortho = dot(columns[:, rows], factors[q], ((0,), (0,)))
             fresh = (weights[q, rows, :].astype(jnp.float32) - factor * ortho).astype(jnp.bfloat16)
             made[q][pl.ds(y * group, group)] = fresh.reshape(group, piece, fresh.shape[1])
             lax.fori_loop(jnp.where(dy == 0, 1, dy * group), (dy + 1) * group, spread, 0)
@@ -390,7 +433,7 @@
 
         def collect(k, carry, q=q):
             to = shifted(me, k)
-            ready[q][k] = held[q][inverse[to]]
+            ready[q][k] = held[q][inverse[0, to]]
             pltpu.make_async_remote_copy(
                 src_ref=ready[q].at[k], dst_ref=outs[q].at[me], send_sem=send.at[2 + q], recv_sem=recv.at[2 + q],
                 device_id={"ep": to}, device_id_type=MESH,
@@ -398,7 +441,7 @@
             return carry
 
         lax.fori_loop(1, n, collect, 0)
-        ready[q][0] = held[q][inverse[me]]
+        ready[q][0] = held[q][inverse[0, me]]
         pltpu.make_async_copy(ready[q].at[0], outs[q].at[me], local.at[2 + q]).start()
 
     trade.wait_send()
@@ -420,13 +463,17 @@
     half, inner = gate.shape
     pieces = (n, half // n, inner)
     shape = jax.ShapeDtypeStruct(pieces, gate.dtype)
-    everywhere, vmem = pl.BlockSpec(memory_space=pl.ANY), pl.BlockSpec(memory_space=pltpu.VMEM)
+    everywhere = pl.BlockSpec(memory_space=pl.ANY)
     return pl.pallas_call(
         functools.partial(move_kernel, n, factor),
         out_shape=(shape, shape),
-        in_specs=[pl.BlockSpec(memory_space=pltpu.SMEM), vmem, vmem, vmem, everywhere, everywhere],
+        in_specs=[everywhere] * 6,
         out_specs=(everywhere, everywhere),
         scratch_shapes=[
+            pltpu.SMEM(inverse.shape, jnp.int32),
+            pltpu.VMEM(kernel_matrix.shape, jnp.float32),
+            pltpu.VMEM(rows.shape, rows.dtype),
+            pltpu.VMEM(columns.shape, columns.dtype),
             pltpu.VMEM((2, half, inner), gate.dtype),
             pltpu.VMEM((2,) + rows.shape, rows.dtype),
         ]
@@ -437,9 +484,10 @@
             pltpu.SemaphoreType.DMA((4,)),
             pltpu.SemaphoreType.DMA((4,)),
             pltpu.SemaphoreType.DMA((2,)),
+            pltpu.SemaphoreType.DMA((4,)),
         ],
         compiler_params=pltpu.CompilerParams(
-            collective_id=2, has_side_effects=True, vmem_limit_bytes=48 * 2**20
+            collective_id=2, has_side_effects=True, vmem_limit_bytes=63 * 2**20
         ),
         name="move",
     )(inverse, kernel_matrix, rows, columns, gate, up)
@@ -467,7 +515,7 @@
         expert_ids.T, copy_choice.T, probs.T, new_owner.reshape(1, experts), dy, saved_inputs[0, 0],
         saved_gate[0, 0], saved_up[0, 0], down_weight[0],
     )
-    factor_rows, columns, inverse = rows.reshape(-1, inner), columns.reshape(-1, half), inverse.reshape(experts)
+    factor_rows, columns = rows.reshape(-1, inner), columns.reshape(-1, half)
     own, other = move(
         experts, step_scale * math.sqrt(width), inverse, kernel_matrix, factor_rows, columns, gate_weight[0], up_weight[0]
     )

time: 195 us -> 192 us (0.985)
  local copies, waits for them, and re-layouts: 6.83 us -> 0 us
  Pallas kernels: 185 us -> 188 us
    unnamed x16 -> x0, local copies, waits for them, and re-layouts: 6.83 us -> none
    pallas_call x1, Pallas kernels: 36.1 us -> 39.1 us  [route(): pl.pallas_call(functools.partial(route_kernel, top), out_shape=(jax.Shape...]
where the time goes in v3:
time: 192 us
  Pallas kernels  188 us (98%)
  other arithmetic  3.75 us (2%)
    pallas_call x1, Pallas kernels, move(): pl.pallas_call(functools.partial(move_kernel, n, factor), out_shape=(shap...  148 us
    pallas_call x1, Pallas kernels, route(): pl.pallas_call(functools.partial(route_kernel, top), out_shape=(jax.Shape...  39.1 us

profile of v3, /device:TPU:1, one launch (start us, length us, event | category | flops | bytes accessed | tf_op | source)
XLA Modules:
  0.0 192.0 jit_solution(17306525667681702184)
XLA Ops:
  0.6 39.1 %route.1 = (f32[512,512]{1,0:T(8,128)}, bf16[2,256,768]{2,1,0:T(8,128)(2,1)}, bf16[2,256,1024]{2,1,0:T(8,128)(2,1)}, s32[1,128]{1,0:T(1,128)}) custom-call(s32[8,32]{1,0:T(8,128)} %bitcast.24, s32[8,32]{1,0:T(8,128)} %bitcast.25, f32[8,32]{1,0:T(8,128)} %bitcast.26, s32[1,128]{1,0:T(1,128)} %bitcast.27, bf16[32,2048]{1,0:T(8,128)(2,1)} %dy_ref.1, ...), custom_call_target="tpu_custom_call" | custom-call | tf_op jit(solution)/shard_map/route/pallas_call | solution.py:282
  39.7 148.5 %move.1 = (bf16[128,8,768]{2,1,0:T(8,128)(2,1)}, bf16[128,8,768]{2,1,0:T(8,128)(2,1)}) custom-call(s32[1,128]{1,0:T(1,128)} %get-tuple-element.8.inverse_ref, f32[512,512]{1,0:T(8,128)} %get-tuple-element.9.k_ref, bf16[512,768]{1,0:T(8,128)(2,1)} %bitcast.21, bf16[512,1024]{1,0:T(8,128)(2,1)} %bitcast.20, bf16[1024,768]{1,0:T(8,128)(2,1)} %bitcast.17, ...), custom_call_target="tpu_custom_call" | custom-call | tf_op jit(solution)/shard_map/move/pallas_call | solution.py:467
  188.2 3.8 %select_bitcast_fusion = (bf16[1,1024,768]{2,1,0:T(8,128)(2,1)}, bf16[1,1024,768]{2,1,0:T(8,128)(2,1)}) fusion(bf16[128,8,768]{2,1,0:T(8,128)(2,1)} %get-tuple-element.13, bf16[128,8,768]{2,1,0:T(8,128)(2,1)} %get-tuple-element.12, pred[]{:T(512)S(6)} %eq.3), kind=kLoop, calls=%fused_computation | loop fusion | flops 1572864 | bytes 6291457 | tf_op jit(solution)/shard_map/reshape | solution.py:523

commit v4 on v3

--- a/solution.py
+++ b/solution.py
@@ -84,12 +84,36 @@
     )
 
 
-def route_kernel(
-    top, ids_ref, copy_ref, probs_ref, owner_ref, dy_ref, x_ref, g_ref, u_ref, down_ref, k_out, r_out, x_out, inverse_out,
-    ids, copies_of, probs, owners, products, slices, spread_of,
+def orthogonal_factor(kernel_matrix, rows):
+    high = kernel_matrix.astype(jnp.bfloat16)
+    low = (kernel_matrix - high.astype(jnp.float32)).astype(jnp.bfloat16)
+    scale = None
+    for repeat in range(ITERS):
+        square = dot(rows, rows, ((1,), (1,)))
+        if not repeat:
+            total = jnp.sqrt(jnp.maximum(jnp.sum(square * kernel_matrix), 0.0))
+            scale = 1.0 / (total + epsilon)
+            square = square * (scale * scale)
+        square = square.astype(jnp.bfloat16)
+        gram = dot(square, high, ((1,), (0,))) + dot(square, low, ((1,), (0,)))
+        half = gram.astype(jnp.bfloat16)
+        poly = quintic_second * gram + quintic_third * dot(half, half, ((1,), (0,)))
+        mixed = quintic_first * rows.astype(jnp.float32) + dot(poly.astype(jnp.bfloat16), rows, ((1,), (0,)))
+        if not repeat:
+            mixed = mixed * scale
+        rows = mixed.astype(jnp.bfloat16)
+    return rows
+
+
+def step_kernel(
+    top, factor, ids_ref, copy_ref, probs_ref, inverse_ref, dy_ref, x_ref, g_ref, u_ref, down_ref, gate_ref, up_ref,
+    own_out, other_out,
+    ids, copies_of, probs, products, slices,
     line, meta, gates, keys, sent, routed, raw, inputs, down, rows, other,
     line_send, line_recv, keys_sem, plane_send, plane_recv, near_send, near_recv, pair_send, pair_recv,
-    own_sem, piece_sem, small_sem, out_sem,
+    own_sem, piece_sem, small_sem,
+    inverse, weights, factors, made0, made1, held0, held1, ready0, ready1,
+    load, send, recv, local, swap_sem, index_sem,
 ):
     me = lax.axis_index("ep")
     core = lax.axis_index("rep")
@@ -108,11 +132,13 @@
     small = [
         pltpu.make_async_copy(src, dst, small_sem.at[i])
         for i, (src, dst) in enumerate(
-            ((ids_ref, ids), (copy_ref, copies_of), (probs_ref, probs), (owner_ref, owners))
+            ((ids_ref, ids), (copy_ref, copies_of), (probs_ref, probs))
         )
     ]
     for copy in small:
         copy.start()
+    indices = pltpu.make_async_copy(inverse_ref, inverse, index_sem)
+    indices.start()
     barrier = pltpu.get_barrier_semaphore()
 
     def greet_line(k, carry):
@@ -139,13 +165,19 @@
     own.append(pltpu.make_async_copy(down_ref, down.at[core], own_sem.at[CHUNKS + 2]))
     own.append(pltpu.make_async_copy(g_ref, gates.at[0], own_sem.at[CHUNKS + 3]))
     own.append(pltpu.make_async_copy(u_ref, gates.at[1], own_sem.at[CHUNKS + 4]))
-    for copy in small[:3]:
+    for copy in small:
         copy.wait()
     keyed = (ids[...] * 2 + copies_of[...]).astype(jnp.float32)
     packed = jnp.concatenate([keyed, probs[...]], axis=0)
     meta[...] = jnp.concatenate([packed, jnp.zeros((2 * top, 128 - count), jnp.float32)], axis=1)
     for copy in own:
         copy.start()
+    for c, refs in enumerate(((gate_ref, up_ref), (up_ref, gate_ref))):
+        @pl.when(core == c)
+        def _(refs=refs):
+            for q in range(2):
+                pltpu.make_async_copy(refs[q], weights.at[q], load.at[q]).start()
+
     pl.semaphore_wait(barrier, nz + 2 * (spots - 1))
 
     def send_keys(k, carry):
@@ -212,20 +244,6 @@
     own[CHUNKS + 4].wait()
     gate_value = gates[0].astype(jnp.float32).reshape(pairs, g_ref.shape[-1])
     up_value = gates[1].astype(jnp.float32).reshape(pairs, u_ref.shape[-1])
-    experts = owner_ref.shape[1]
-    low = lax.broadcasted_iota(jnp.int32, (experts, experts), 0)
-    wide = lax.broadcasted_iota(jnp.int32, (experts, experts), 1).astype(jnp.float32)
-    small[3].wait()
-    held = jnp.sum(jnp.where(owners[...] == low, wide, 0.0), axis=1, keepdims=True)
-    spread_of[...] = jnp.broadcast_to(held, (experts, experts)).T[:1].astype(jnp.int32)
-    outgoing = [
-        pltpu.make_async_copy(src, dst, out_sem.at[i])
-        for i, (src, dst) in enumerate(
-            ((products, k_out), (slices, x_out), (spread_of, inverse_out), (rows, r_out))
-        )
-    ]
-    for copy in outgoing[:3]:
-        copy.start()
     own[CHUNKS + 2].wait()
     swaps[1].wait_recv()
     near = pl.ds(0, spots - 1)
@@ -248,156 +266,26 @@
     first = core == 0
     rows[core] = jnp.where(first, gate_rows, up_rows).astype(jnp.bfloat16)
     other[...] = jnp.where(first, up_rows, gate_rows).astype(jnp.bfloat16)
-    last = remote(other, rows.at[core], pair_send.at[2], pair_recv.at[2], partner)
-    last.start()
-
-    last.wait_recv()
-    outgoing[3].start()
-    all_keys.wait_send()
-    for swap in swaps:
-        swap.wait_send()
-    for h in range(CHUNKS):
-        remote(line.at[h, others], line.at[h, others], line_send.at[h], line_recv.at[h], above(1)).wait_send()
-        remote(
-            sent.at[h, 1 - core, spot], routed.at[spot, :, columns(h)], near_send.at[h], near_recv.at[h], partner
-        ).wait_send()
-        both = sent.at[h, :, near]
-        remote(both, both, plane_send.at[h], plane_recv.at[h], partner).wait_send()
-    last.wait_send()
-    for copy in outgoing:
-        copy.wait()
-
-
-def route(ids, copies, probs, owner, dy, inputs, gate, up, down):
-    top = ids.shape[0]
-    pairs, features = inputs.shape[0] * inputs.shape[1], inputs.shape[2]
-    inner, half = down.shape
-    tokens = dy.shape[0]
-    nz, spots = GRID[2], GRID[0] * GRID[1]
-    slots = pairs // spots
-    width = half // CHUNKS
-    everywhere = pl.BlockSpec(memory_space=pl.ANY)
-    bf16 = jnp.bfloat16
-    semaphores = pltpu.SemaphoreType.DMA
-    return pl.pallas_call(
-        functools.partial(route_kernel, top),
-        out_shape=(
-            jax.ShapeDtypeStruct((2 * pairs, 2 * pairs), jnp.float32),
-            jax.ShapeDtypeStruct((2, pairs, inner), bf16),
-            jax.ShapeDtypeStruct((2, pairs, half), bf16),
-            jax.ShapeDtypeStruct(owner.shape, jnp.int32),
-        ),
-        in_specs=[everywhere] * 9,
-        out_specs=(everywhere,) * 4,
-        scratch_shapes=[
-            pltpu.VMEM(ids.shape, jnp.int32),
-            pltpu.VMEM(ids.shape, jnp.int32),
-            pltpu.VMEM(ids.shape, jnp.float32),
-            pltpu.VMEM(owner.shape, jnp.int32),
-            pltpu.VMEM((2 * pairs, 2 * pairs), jnp.float32),
-            pltpu.VMEM((2, pairs, half), bf16),
-            pltpu.VMEM(owner.shape, jnp.int32),
-            pltpu.VMEM((CHUNKS, nz, tokens, width), bf16),
-            pltpu.VMEM((2 * top, 128), jnp.float32),
-            pltpu.VMEM((2,) + gate.shape, bf16),
-            pltpu.VMEM((nz, 2 * top, 128), jnp.float32),
-            pltpu.VMEM((CHUNKS, 2, spots, slots, width), bf16),
-            pltpu.VMEM((spots, slots, features), bf16),
-            pltpu.VMEM((2,) + inputs.shape, bf16),
-            pltpu.VMEM((2, pairs, features), bf16),
-            pltpu.VMEM((2, inner, half), bf16),
-            pltpu.VMEM((2, pairs, inner), bf16),
-            pltpu.VMEM((pairs, inner), bf16),
-            semaphores((CHUNKS,)),
-            semaphores((CHUNKS,)),
-            semaphores((2,)),
-            semaphores((CHUNKS,)),
-            semaphores((CHUNKS,)),
-            semaphores((CHUNKS,)),
-            semaphores((CHUNKS,)),
-            semaphores((3,)),
-            semaphores((3,)),
-            semaphores((CHUNKS + 5,)),
-            semaphores((CHUNKS,)),
-            semaphores((4,)),
-            semaphores((4,)),
-        ],
-        compiler_params=pltpu.CompilerParams(
-            collective_id=1, has_side_effects=True, vmem_limit_bytes=63 * 2**20
-        ),
-        name="route",
-    )(ids, copies, probs, owner, dy, inputs, gate, up, down)
-
-
-def orthogonal_factor(kernel_matrix, rows):
-    high = kernel_matrix.astype(jnp.bfloat16)
-    low = (kernel_matrix - high.astype(jnp.float32)).astype(jnp.bfloat16)
-    scale = None
-    for repeat in range(ITERS):
-        square = dot(rows, rows, ((1,), (1,)))
-        if not repeat:
-            total = jnp.sqrt(jnp.maximum(jnp.sum(square * kernel_matrix), 0.0))
-            scale = 1.0 / (total + epsilon)
-            square = square * (scale * scale)
-        square = square.astype(jnp.bfloat16)
-        gram = dot(square, high, ((1,), (0,))) + dot(square, low, ((1,), (0,)))
-        half = gram.astype(jnp.bfloat16)
-        poly = quintic_second * gram + quintic_third * dot(half, half, ((1,), (0,)))
-        mixed = quintic_first * rows.astype(jnp.float32) + dot(poly.astype(jnp.bfloat16), rows, ((1,), (0,)))
-        if not repeat:
-            mixed = mixed * scale
-        rows = mixed.astype(jnp.bfloat16)
-    return rows
-
-
-def move_kernel(
-    n, factor, inverse_ref, k_ref, r_ref, x_ref, gate_ref, up_ref, own_out, other_out,
-    inverse, products, begin, columns, weights, factors, made0, made1, held0, held1, ready0, ready1, load, send, recv, local, swap, fetch,
-):
-    me = lax.axis_index("ep")
-    core = lax.axis_index("rep")
+    swapped = remote(other, rows.at[core], pair_send.at[2], pair_recv.at[2], partner)
+    swapped.start()
+
+    swapped.wait_recv()
+
+    n = made0.shape[0]
     outs, made, held, ready = (own_out, other_out), (made0, made1), (held0, held1), (ready0, ready1)
     ny = GRID[0]
     group = n // ny
     piece = weights.shape[1] // n
     block = group * piece
     rest = pl.ds(0, n - 1)
-    partner = {"rep": 1 - core}
-
-    fetches = [
-        pltpu.make_async_copy(src, dst, fetch.at[i])
-        for i, (src, dst) in enumerate(
-            ((k_ref, products), (r_ref, begin), (x_ref, columns), (inverse_ref, inverse))
-        )
-    ]
-    for copy in fetches:
-        copy.start()
-    barrier = pltpu.get_barrier_semaphore()
-
-    def say(k, carry):
-        pl.semaphore_signal(barrier, inc=1, device_id={"ep": shifted(me, k)}, device_id_type=MESH)
-        return carry
-
-    lax.fori_loop(1, n, say, 0)
-    pl.semaphore_signal(barrier, inc=1, device_id=partner, device_id_type=MESH)
-
-    for c, refs in enumerate(((gate_ref, up_ref), (up_ref, gate_ref))):
-        @pl.when(core == c)
-        def _(refs=refs):
-            for q in range(2):
-                pltpu.make_async_copy(refs[q], weights.at[q], load.at[q]).start()
-
-    fetches[0].wait()
-    fetches[1].wait()
-    factors[0] = orthogonal_factor(products[...], begin[...])
-    pl.semaphore_wait(barrier, n)
+
+    factors[0] = orthogonal_factor(products[...], rows[...].reshape(2 * pairs, rows.shape[2]))
     trade = pltpu.make_async_remote_copy(
-        src_ref=factors.at[0], dst_ref=factors.at[1], send_sem=swap.at[0], recv_sem=swap.at[1],
+        src_ref=factors.at[0], dst_ref=factors.at[1], send_sem=swap_sem.at[0], recv_sem=swap_sem.at[1],
         device_id=partner, device_id_type=MESH,
     )
     trade.start()
-    fetches[2].wait()
-    fetches[3].wait()
+    indices.wait()
 
     for q in range(2):
         pltpu.make_async_copy(gate_ref, weights.at[q], load.at[q]).wait()
@@ -414,9 +302,9 @@
 
         def produce(dy, carry, q=q):
             y = lax.rem(me // group + dy, ny)
-            rows = pl.ds(pl.multiple_of(y * block, block), block)
-            ortho = dot(columns[:, rows], factors[q], ((0,), (0,)))
-            fresh = (weights[q, rows, :].astype(jnp.float32) - factor * ortho).astype(jnp.bfloat16)
+            span = pl.ds(pl.multiple_of(y * block, block), block)
+            ortho = dot(slices[:, :, span].reshape(2 * pairs, block), factors[q], ((0,), (0,)))
+            fresh = (weights[q, span, :].astype(jnp.float32) - factor * ortho).astype(jnp.bfloat16)
             made[q][pl.ds(y * group, group)] = fresh.reshape(group, piece, fresh.shape[1])
             lax.fori_loop(jnp.where(dy == 0, 1, dy * group), (dy + 1) * group, spread, 0)
             return carry
@@ -458,39 +346,84 @@
         last.wait_send()
         last.wait_recv()
 
-
-def move(n, factor, inverse, kernel_matrix, rows, columns, gate, up):
-    half, inner = gate.shape
-    pieces = (n, half // n, inner)
-    shape = jax.ShapeDtypeStruct(pieces, gate.dtype)
+    all_keys.wait_send()
+    for swap in swaps:
+        swap.wait_send()
+    for h in range(CHUNKS):
+        remote(line.at[h, others], line.at[h, others], line_send.at[h], line_recv.at[h], above(1)).wait_send()
+        remote(
+            sent.at[h, 1 - core, spot], routed.at[spot, :, columns(h)], near_send.at[h], near_recv.at[h], partner
+        ).wait_send()
+        both = sent.at[h, :, near]
+        remote(both, both, plane_send.at[h], plane_recv.at[h], partner).wait_send()
+    swapped.wait_send()
+
+
+def step(factor, ids, copies, probs, inverse, dy, inputs, gate, up, down, gate_matrix, up_matrix):
+    top = ids.shape[0]
+    pairs, features = inputs.shape[0] * inputs.shape[1], inputs.shape[2]
+    inner, half = down.shape
+    tokens = dy.shape[0]
+    nz, spots = GRID[2], GRID[0] * GRID[1]
+    slots = pairs // spots
+    width = half // CHUNKS
     everywhere = pl.BlockSpec(memory_space=pl.ANY)
+    bf16 = jnp.bfloat16
+    experts = inverse.shape[1]
+    shape = jax.ShapeDtypeStruct((experts, half // experts, inner), bf16)
+    semaphores = pltpu.SemaphoreType.DMA
     return pl.pallas_call(
-        functools.partial(move_kernel, n, factor),
+        functools.partial(step_kernel, top, factor),
         out_shape=(shape, shape),
-        in_specs=[everywhere] * 6,
+        in_specs=[everywhere] * 11,
         out_specs=(everywhere, everywhere),
         scratch_shapes=[
+            pltpu.VMEM(ids.shape, jnp.int32),
+            pltpu.VMEM(ids.shape, jnp.int32),
+            pltpu.VMEM(ids.shape, jnp.float32),
+            pltpu.VMEM((2 * pairs, 2 * pairs), jnp.float32),
+            pltpu.VMEM((2, pairs, half), bf16),
+            pltpu.VMEM((CHUNKS, nz, tokens, width), bf16),
+            pltpu.VMEM((2 * top, 128), jnp.float32),
+            pltpu.VMEM((2,) + gate.shape, bf16),
+            pltpu.VMEM((nz, 2 * top, 128), jnp.float32),
+            pltpu.VMEM((CHUNKS, 2, spots, slots, width), bf16),
+            pltpu.VMEM((spots, slots, features), bf16),
+            pltpu.VMEM((2,) + inputs.shape, bf16),
+            pltpu.VMEM((2, pairs, features), bf16),
+            pltpu.VMEM((2, inner, half), bf16),
+            pltpu.VMEM((2, pairs, inner), bf16),
+            pltpu.VMEM((pairs, inner), bf16),
+            semaphores((CHUNKS,)),
+            semaphores((CHUNKS,)),
+            semaphores((2,)),
+            semaphores((CHUNKS,)),
+            semaphores((CHUNKS,)),
+            semaphores((CHUNKS,)),
+            semaphores((CHUNKS,)),
+            semaphores((3,)),
+            semaphores((3,)),
+            semaphores((CHUNKS + 5,)),
+            semaphores((CHUNKS,)),
+            semaphores((3,)),
             pltpu.SMEM(inverse.shape, jnp.int32),
-            pltpu.VMEM(kernel_matrix.shape, jnp.float32),
-            pltpu.VMEM(rows.shape, rows.dtype),
-            pltpu.VMEM(columns.shape, columns.dtype),
-            pltpu.VMEM((2, half, inner), gate.dtype),
-            pltpu.VMEM((2,) + rows.shape, rows.dtype),
+            pltpu.VMEM((2, half, inner), bf16),
+            pltpu.VMEM((2, 2 * pairs, inner), bf16),
         ]
-        + [pltpu.VMEM(pieces, gate.dtype)] * 6
+        + [pltpu.VMEM(shape.shape, bf16)] * 6
         + [
-            pltpu.SemaphoreType.DMA((2,)),
-            pltpu.SemaphoreType.DMA((4,)),
-            pltpu.SemaphoreType.DMA((4,)),
-            pltpu.SemaphoreType.DMA((4,)),
-            pltpu.SemaphoreType.DMA((2,)),
-            pltpu.SemaphoreType.DMA((4,)),
+            semaphores((2,)),
+            semaphores((4,)),
+            semaphores((4,)),
+            semaphores((4,)),
+            semaphores((2,)),
+            semaphores,
         ],
         compiler_params=pltpu.CompilerParams(
-            collective_id=2, has_side_effects=True, vmem_limit_bytes=63 * 2**20
+            collective_id=1, has_side_effects=True, vmem_limit_bytes=60 * 2**20
         ),
-        name="move",
-    )(inverse, kernel_matrix, rows, columns, gate, up)
+        name="step",
+    )(ids, copies, probs, inverse, dy, inputs, gate, up, down, gate_matrix, up_matrix)
 
 
 def shards(
@@ -511,13 +444,13 @@
     width = dy.shape[1]
     inner = saved_gate.shape[4]
     half = width // 2
-    kernel_matrix, rows, columns, inverse = route(
-        expert_ids.T, copy_choice.T, probs.T, new_owner.reshape(1, experts), dy, saved_inputs[0, 0],
-        saved_gate[0, 0], saved_up[0, 0], down_weight[0],
-    )
-    factor_rows, columns = rows.reshape(-1, inner), columns.reshape(-1, half)
-    own, other = move(
-        experts, step_scale * math.sqrt(width), inverse, kernel_matrix, factor_rows, columns, gate_weight[0], up_weight[0]
+    expert = jnp.arange(experts, dtype=jnp.int32)
+    inverse = jnp.sum(
+        jnp.where(new_owner[:, None] == expert[None, :], expert[:, None], 0), axis=0, dtype=jnp.int32
+    ).reshape(1, experts)
+    own, other = step(
+        step_scale * math.sqrt(width), expert_ids.T, copy_choice.T, probs.T, inverse, dy,
+        saved_inputs[0, 0], saved_gate[0, 0], saved_up[0, 0], down_weight[0], gate_weight[0], up_weight[0],
     )
     new_gate, new_up = jnp.where(first, own, other), jnp.where(first, other, own)
     return new_gate.reshape(1, half, inner), new_up.reshape(1, half, inner)

time: 192 us -> 186 us (0.969)
  Pallas kernels: 188 us -> 180 us
    pallas_call x2 -> x1, Pallas kernels: 188 us -> 180 us  [step(): pl.pallas_call(functools.partial(step_kernel, top, factor), out_shape=(sh...]
where the time goes in v4:
time: 186 us
  Pallas kernels  180 us (97%)
  other arithmetic  5.02 us (3%)
    pallas_call x1, Pallas kernels, step(): pl.pallas_call(functools.partial(step_kernel, top, factor), out_shape=(sh...  180 us
    reshape x1, other arithmetic, shards(): return (new_gate.reshape(1, half, inner), new_up.reshape(1, half, inner))  3.75 us

profile of v4, /device:TPU:1, one launch (start us, length us, event | category | flops | bytes accessed | tf_op | source)
XLA Modules:
  0.0 186.2 jit_solution(6093529571676013736)
XLA Ops:
  0.6 1.3 select_reduce_fusion
  1.9 180.5 %step.1 = (bf16[128,8,768]{2,1,0:T(8,128)(2,1)}, bf16[128,8,768]{2,1,0:T(8,128)(2,1)}) custom-call(s32[8,32]{1,0:T(8,128)} %bitcast.20, s32[8,32]{1,0:T(8,128)} %bitcast.21, f32[8,32]{1,0:T(8,128)} %bitcast.22, s32[1,128]{1,0:T(1,128)} %bitcast.23, bf16[32,2048]{1,0:T(8,128)(2,1)} %dy_ref.1, bf16[128,2,2048]{2,1,0:T(2,128)(2,1)} %bitcast.17, ...), custom_call_target="tpu_custom_call" | custom-call | tf_op jit(solution)/shard_map/step/pallas_call | solution.py:375
  182.4 3.8 %select_bitcast_fusion = (bf16[1,1024,768]{2,1,0:T(8,128)(2,1)}, bf16[1,1024,768]{2,1,0:T(8,128)(2,1)}) fusion(bf16[128,8,768]{2,1,0:T(8,128)(2,1)} %get-tuple-element.5, bf16[128,8,768]{2,1,0:T(8,128)(2,1)} %get-tuple-element.4, pred[]{:T(512)S(6)} %eq.16), kind=kLoop, calls=%fused_computation | loop fusion | flops 1572864 | bytes 6291457 | tf_op jit(solution)/shard_map/reshape | solution.py:456

commit v5 on v4

--- a/solution.py
+++ b/solution.py
@@ -172,12 +172,6 @@
     meta[...] = jnp.concatenate([packed, jnp.zeros((2 * top, 128 - count), jnp.float32)], axis=1)
     for copy in own:
         copy.start()
-    for c, refs in enumerate(((gate_ref, up_ref), (up_ref, gate_ref))):
-        @pl.when(core == c)
-        def _(refs=refs):
-            for q in range(2):
-                pltpu.make_async_copy(refs[q], weights.at[q], load.at[q]).start()
-
     pl.semaphore_wait(barrier, nz + 2 * (spots - 1))
 
     def send_keys(k, carry):
@@ -199,6 +193,13 @@
     ]
     for swap in swaps:
         swap.start()
+
+    for c, refs in enumerate(((gate_ref, up_ref), (up_ref, gate_ref))):
+        @pl.when(core == c)
+        def _(refs=refs):
+            for q in range(2):
+                pltpu.make_async_copy(refs[q], weights.at[q], load.at[q]).start()
+
 
     others = pl.ds(0, nz - 1)
     all_keys = remote(keys.at[others], keys.at[others], keys_sem.at[0], keys_sem.at[1], above(1))

time: 186 us -> 186 us (level)
  no operation moved by 1% of the time
where the time goes in v5:
time: 186 us
  Pallas kernels  180 us (97%)
  other arithmetic  5.02 us (3%)
    pallas_call x1, Pallas kernels, step(): pl.pallas_call(functools.partial(step_kernel, top, factor), out_shape=(sh...  180 us
    reshape x1, other arithmetic, shards(): return (new_gate.reshape(1, half, inner), new_up.reshape(1, half, inner))  3.75 us

profile of v5, /device:TPU:1, one launch (start us, length us, event | category | flops | bytes accessed | tf_op | source)
XLA Modules:
  0.0 186.2 jit_solution(9800341603658569765)
XLA Ops:
  0.6 1.3 select_reduce_fusion
  1.9 180.5 %step.1 = (bf16[128,8,768]{2,1,0:T(8,128)(2,1)}, bf16[128,8,768]{2,1,0:T(8,128)(2,1)}) custom-call(s32[8,32]{1,0:T(8,128)} %bitcast.20, s32[8,32]{1,0:T(8,128)} %bitcast.21, f32[8,32]{1,0:T(8,128)} %bitcast.22, s32[1,128]{1,0:T(1,128)} %bitcast.23, bf16[32,2048]{1,0:T(8,128)(2,1)} %dy_ref.1, bf16[128,2,2048]{2,1,0:T(2,128)(2,1)} %bitcast.17, ...), custom_call_target="tpu_custom_call" | custom-call | tf_op jit(solution)/shard_map/step/pallas_call | solution.py:376
  182.4 3.8 %select_bitcast_fusion = (bf16[1,1024,768]{2,1,0:T(8,128)(2,1)}, bf16[1,1024,768]{2,1,0:T(8,128)(2,1)}) fusion(bf16[128,8,768]{2,1,0:T(8,128)(2,1)} %get-tuple-element.5, bf16[128,8,768]{2,1,0:T(8,128)(2,1)} %get-tuple-element.4, pred[]{:T(512)S(6)} %eq.16), kind=kLoop, calls=%fused_computation | loop fusion | flops 1572864 | bytes 6291457 | tf_op jit(solution)/shard_map/reshape | solution.py:457
